TPU v7x, 32 devices: a whole 2x2x4 slice. The times are simulated.
32 devices in a mesh: swath: 2 (over x), band: 16 (over z, y, core).
Axes of the slice: x: 2, y: 2, z: 4, core: 2. Of those that a mesh axis runs over, the one named last changes fastest.
Arguments:
- design: bfloat16 [512, 16384], P(('swath', 'band')), parts along dimension 0, may hold values from 0 to 1
- row_taps: bfloat16 [8, 33], replicated, may hold values from -1 to 1
- column_taps: bfloat16 [8, 33], replicated, may hold values from -1 to 1
- kernel_weight: float32 [8], replicated, may hold values from 0.5 to 2
- interp: bfloat16 [32, 8], replicated, may hold values from 0 to 0.29882812
- block_shift: int32 [2, 4, 16], P(None, 'swath', 'band'), parts along dimension 1, may hold values from -24 to 24
- block_phase: int32 [2, 4, 16], P(None, 'swath', 'band'), parts along dimension 1, may hold values from 0 to 31
- care: int32 [4, 16], P('swath', 'band'), parts along dimension 0, may hold values 0 or 1
- image: bfloat16 [512, 16384], P('swath', 'band'), parts along dimension 0, may hold values from 0 to 20, as said below
Outputs:
- diff_map: bfloat16 [512, 16384], P('swath', 'band'), parts along dimension 0
There are 2 independent parts, one for each index of `swath`. A program takes and returns all parts, laid end to end along the dimension named above; an argument that names none is the same for every part. Nothing has to cross between parts.
Inputs may be any that keep to these rules, and one draw needn't show every extreme that they name: `image`: nonnegative intensities.
All inputs are finite; a program needn't handle non-finite values. No bound on the sum of `care` on one device may be relied on, other than what follows from the above.
Results may differ from a plain program's by a relative error of at most 0.0045.
Values may be sent and summed in bfloat16 or wider, within the bound.
No kernel may reach another device: no remote copies, remote signals or barrier semaphores. Data moves between devices by JAX's collectives and lax.ppermute only.
A program may use at most 64 MiB of HBM per device.

v0:
```python
import jax
import jax.numpy as jnp
from jax import lax
from jax.sharding import PartitionSpec as P

NK = 8
KH = 16
IH = 4
NF = 32
BLK = 128
P_SIZE = 28


epsilon = 1e-05
panel = 128


def padded_2(cells, sides, width):
    for axis, dim in sides:
        count = lax.axis_size(axis)
        ends = count - 1
        head = lax.slice_in_dim(cells, 0, width, axis=dim)
        tail = lax.slice_in_dim(cells, cells.shape[dim] - width, cells.shape[dim], axis=dim)
        cells = jnp.concatenate(
            [
                lax.ppermute(tail, axis, [(i, (i + 1) % count) for i in range(ends)]),
                cells,
                lax.ppermute(head, axis, [((i + 1) % count, i) for i in range(ends)]),
            ],
            axis=dim,
        )
    return cells


def band_matrix(offsets, phases, interp, size_out, size_in):
    table = jax.nn.one_hot(phases, NF, dtype=jnp.float32)
    weights = jnp.dot(table, interp.astype(jnp.float32), precision=lax.Precision.HIGHEST)
    outer = jnp.arange(size_out, dtype=jnp.int32)
    inner = jnp.arange(size_in, dtype=jnp.int32)
    position = (
        inner[None, None, :] - outer[None, :, None] - offsets[:, None, None] + (IH - 1 - P_SIZE)
    )
    matrix = jnp.zeros(position.shape, jnp.float32)
    for tap in range(2 * IH):
        matrix = matrix + jnp.where(position == tap, weights[:, tap][:, None, None], 0.0)
    return matrix.astype(jnp.bfloat16)


def warp_strip(framed, shifts, phases, interp):
    height = framed.shape[0] - BLK - 2 * P_SIZE
    across = framed.shape[1]
    strip_cols = across - 2 * P_SIZE
    count = height // BLK
    upper = framed[:height].reshape(count, BLK, across)[:, :P_SIZE]
    middle = framed[P_SIZE : P_SIZE + height].reshape(count, BLK, across)
    lower = framed[BLK + P_SIZE : BLK + P_SIZE + height].reshape(count, BLK, across)[:, :P_SIZE]
    blocks = jnp.concatenate([upper, middle, lower], axis=1)
    row_matrix = band_matrix(shifts[0], phases[0], interp, BLK, BLK + 2 * P_SIZE)
    column_matrix = band_matrix(shifts[1], phases[1], interp, strip_cols, across)
    partial_value = jnp.einsum(
        "brs,bsc->brc", row_matrix, blocks, preferred_element_type=jnp.float32
    ).astype(jnp.bfloat16)
    return jnp.einsum(
        "brs,bcs->brc", partial_value, column_matrix, preferred_element_type=jnp.float32
    )


def on_device(
    design, row_taps, column_taps, kernel_weight, interp, block_shift, block_phase, care, image
):
    devices = lax.axis_size("band")
    rows_dev, width = design.shape
    strip_cols = width // devices
    reach = row_taps.shape[1]
    extended = padded_2(design, (("band", 0),), KH)
    row_offsets = jnp.arange(rows_dev + 2 * KH)[None, :] - jnp.arange(rows_dev)[:, None]
    row_selector = (row_offsets[:, :, None] == jnp.arange(reach)[None, None, :]).astype(
        jnp.bfloat16
    )
    row_mats = jnp.einsum(
        "rst,kt->krs", row_selector, row_taps, preferred_element_type=jnp.float32
    ).astype(jnp.bfloat16)
    window = panel + 2 * KH
    column_offsets = jnp.arange(window)[:, None] - jnp.arange(panel)[None, :]
    column_selector = (column_offsets[:, :, None] == jnp.arange(reach)[None, None, :]).astype(
        jnp.bfloat16
    )
    column_mats = jnp.einsum(
        "ict,kt->kic", column_selector, column_taps, preferred_element_type=jnp.float32
    ).astype(jnp.bfloat16)
    panels = width // panel
    total = jnp.zeros((rows_dev, width), jnp.float32)
    for kernel in range(NK):
        smoothed = jnp.dot(row_mats[kernel], extended, preferred_element_type=jnp.float32).astype(
            jnp.bfloat16
        )
        framed = jnp.pad(smoothed, ((0, 0), (panel, panel))).reshape(rows_dev, panels + 2, panel)
        stacked = jnp.concatenate(
            [framed[:, :-2, panel - KH :], framed[:, 1:-1], framed[:, 2:, :KH]], axis=2
        )
        field = jnp.einsum(
            "rnj,jc->rnc", stacked, column_mats[kernel], preferred_element_type=jnp.float32
        ).reshape(rows_dev, width)
        total = total + kernel_weight[kernel] * field * field
    intensity = total.astype(jnp.bfloat16)
    height = rows_dev * devices
    strip = lax.all_to_all(intensity, "band", split_axis=1, concat_axis=0, tiled=True)
    bordered = padded_2(strip, (("band", 1),), P_SIZE)
    padded = jnp.pad(bordered, ((P_SIZE, BLK + P_SIZE), (0, 0)))
    warped = warp_strip(padded, block_shift[:, :, 0], block_phase[:, :, 0], interp)
    count = height // BLK
    care_blocks = care[:, 0].astype(jnp.float32)
    measured = image.reshape(count, BLK, strip_cols).astype(jnp.float32)
    difference = (care_blocks[:, None, None] * (measured - warped)).reshape(height, strip_cols)
    shifted = jnp.pad(difference, ((1, 1), (0, 0)))
    filtered = difference + 0.5 * (shifted[:-2] + shifted[2:])
    cells = height * width
    first_sum, second_sum = lax.psum((jnp.sum(filtered), jnp.sum(filtered * filtered)), "band")
    mean = first_sum / cells
    variance = second_sum / cells - mean * mean
    centered = filtered - mean
    scaled = (centered * lax.rsqrt(variance + epsilon)).reshape(count, BLK, strip_cols)
    return (care_blocks[:, None, None] * scaled).reshape(height, strip_cols).astype(jnp.bfloat16)


def solution(mesh):
    placed = (
        P(("swath", "band"), None),
        P(),
        P(),
        P(),
        P(),
        P(None, "swath", "band"),
        P(None, "swath", "band"),
        P("swath", "band"),
        P("swath", "band"),
    )
    return jax.shard_map(
        on_device, mesh=mesh, in_specs=placed, out_specs=P("swath", "band"), check_vma=False
    )
```

profile of v0, /device:TPU:0, one launch (start us, length us, event | category | flops | bytes accessed | tf_op | source)
XLA Modules:
  0.0 193.9 jit_solution(986255994731446772)
XLA Ops:
  0.0 2.6 %collective-permute-start = (bf16[16,16384]{1,0:T(8,128)(2,1)}, bf16[16,16384]{1,0:T(8,128)(2,1)S(1)}, u32[]{:S(2)}, u32[]{:S(2)}) collective-permute-start(bf16[16,16384]{1,0:T(8,128)(2,1)} %param.9), channel_id=1, source_target_pairs={{0,1},{1,2},{2,3},{3,4},{4,5},{5,6},{6,7},{7,8},{8,9},{9,10},{10,1... | collective-permute-start | bytes 1572872 | tf_op jit(solution)/shard_map/ppermute | solution.py:26
  8.6 1.6 fusion.215
  35.1 1.5 fusion.34
  39.6 2.5 %fusion.40 = f32[16,128,128]{2,1,0:T(8,128)} fusion(bf16[16,128,16]{1,2,0:T(8,128)(2,1)S(1)} %copy.95, bf16[16,128,128]{1,2,0:T(8,128)(2,1)} %copy.94, bf16[16,128,16]{1,2,0:T(8,128)(2,1)S(1)} %copy.93, bf16[1,160,128]{2,0,1:T(2,128)(2,1)} %get-tuple-element.53), kind=kOutput, calls=%fused_computation.62 | convolution fusion | flops 85852160 | bytes 1744896 | tf_op jit(solution)/shard_map/rnj,jc->rnc/dot_general | solution.py:101
  46.0 2.5 %fusion.46 = f32[16,128,128]{2,1,0:T(8,128)} fusion(bf16[16,128,16]{1,2,0:T(8,128)(2,1)S(1)} %copy.98, bf16[16,128,128]{1,2,0:T(8,128)(2,1)} %copy.97, bf16[16,128,16]{1,2,0:T(8,128)(2,1)S(1)} %copy.96, bf16[1,160,128]{2,0,1:T(2,128)(2,1)} %get-tuple-element.52), kind=kOutput, calls=%fused_computation.68 | convolution fusion | flops 85852160 | bytes 1744896 | tf_op jit(solution)/shard_map/rnj,jc->rnc/dot_general | solution.py:101
  49.9 2.0 %copy.100 = bf16[16,128,128]{1,2,0:T(8,128)(2,1)} copy(bf16[16,128,128]{2,1,0:T(8,128)(2,1)} %slice.326) | data formatting | bytes 1048576
  52.0 1.8 copy.99
  53.8 1.8 copy.101
  55.6 2.6 %fusion.52 = f32[16,128,128]{2,1,0:T(8,128)} fusion(bf16[16,128,16]{1,2,0:T(8,128)(2,1)} %copy.101, bf16[16,128,128]{1,2,0:T(8,128)(2,1)} %copy.100, bf16[16,128,16]{1,2,0:T(8,128)(2,1)} %copy.99, bf16[1,160,128]{2,0,1:T(2,128)(2,1)} %get-tuple-element.51), kind=kOutput, calls=%fused_computation.74 | convolution fusion | flops 85852160 | bytes 1744896 | tf_op jit(solution)/shard_map/rnj,jc->rnc/dot_general | solution.py:101
  58.3 2.4 %reshape.176 = f32[16,16,1024]{2,1,0:T(8,128)} reshape(f32[16,128,128]{2,1,0:T(8,128)} %fusion.52) | data formatting | bytes 2097152 | tf_op jit(solution)/shard_map/reshape | solution.py:103
  60.6 2.1 %copy.103 = bf16[16,128,128]{1,2,0:T(8,128)(2,1)} copy(bf16[16,128,128]{2,1,0:T(8,128)(2,1)} %slice.331) | data formatting | bytes 1048576
  62.7 1.8 copy.102
  64.5 1.8 copy.104
  66.4 2.6 %fusion.58 = f32[16,128,128]{2,1,0:T(8,128)} fusion(bf16[16,128,16]{1,2,0:T(8,128)(2,1)} %copy.104, bf16[16,128,128]{1,2,0:T(8,128)(2,1)} %copy.103, bf16[16,128,16]{1,2,0:T(8,128)(2,1)} %copy.102, bf16[1,160,128]{2,0,1:T(2,128)(2,1)S(1)} %get-tuple-element.50), kind=kOutput, calls=%fused_computation.80 | convolution fusion | flops 85852160 | bytes 1744896 | tf_op jit(solution)/shard_map/rnj,jc->rnc/dot_general | solution.py:101
  68.9 2.4 %reshape.178 = f32[16,16,1024]{2,1,0:T(8,128)} reshape(f32[16,128,128]{2,1,0:T(8,128)} %fusion.58) | data formatting | bytes 2097152 | tf_op jit(solution)/shard_map/reshape | solution.py:103
  71.4 2.0 %copy.106 = bf16[16,128,128]{1,2,0:T(8,128)(2,1)} copy(bf16[16,128,128]{2,1,0:T(8,128)(2,1)} %slice.336) | data formatting | bytes 1048576
  74.6 1.8 copy.107
  76.5 2.6 %fusion.64 = f32[16,128,128]{2,1,0:T(8,128)} fusion(bf16[16,128,16]{1,2,0:T(8,128)(2,1)} %copy.107, bf16[16,128,128]{1,2,0:T(8,128)(2,1)} %copy.106, bf16[16,128,16]{1,2,0:T(8,128)(2,1)S(1)} %copy.105, bf16[1,160,128]{2,0,1:T(2,128)(2,1)S(1)} %get-tuple-element.49), kind=kOutput, calls=%fused_computation.86 | convolution fusion | flops 85852160 | bytes 1744896 | tf_op jit(solution)/shard_map/rnj,jc->rnc/dot_general | solution.py:101
  79.0 2.4 %reshape.180 = f32[16,16,1024]{2,1,0:T(8,128)} reshape(f32[16,128,128]{2,1,0:T(8,128)} %fusion.64) | data formatting | bytes 2097152 | tf_op jit(solution)/shard_map/reshape | solution.py:103
  81.4 2.0 %copy.109 = bf16[16,128,128]{1,2,0:T(8,128)(2,1)} copy(bf16[16,128,128]{2,1,0:T(8,128)(2,1)} %slice.341) | data formatting | bytes 1048576
  85.9 2.5 %fusion.70 = f32[16,128,128]{2,1,0:T(8,128)} fusion(bf16[16,128,16]{1,2,0:T(8,128)(2,1)S(1)} %copy.110, bf16[16,128,128]{1,2,0:T(8,128)(2,1)} %copy.109, bf16[16,128,16]{1,2,0:T(8,128)(2,1)S(1)} %copy.108, bf16[1,160,128]{2,0,1:T(2,128)(2,1)S(1)} %get-tuple-element.48), kind=kOutput, calls=%fused_computation.92 | convolution fusion | flops 85852160 | bytes 1744896 | tf_op jit(solution)/shard_map/rnj,jc->rnc/dot_general | solution.py:101
  88.4 2.4 %reshape.182 = f32[16,16,1024]{2,1,0:T(8,128)} reshape(f32[16,128,128]{2,1,0:T(8,128)} %fusion.70) | data formatting | bytes 2097152 | tf_op jit(solution)/shard_map/reshape | solution.py:103
  90.8 2.0 %copy.112 = bf16[16,128,128]{1,2,0:T(8,128)(2,1)} copy(bf16[16,128,128]{2,1,0:T(8,128)(2,1)} %slice.346) | data formatting | bytes 1048576
  95.2 2.6 %fusion.76 = f32[16,128,128]{2,1,0:T(8,128)} fusion(bf16[16,128,16]{1,2,0:T(8,128)(2,1)S(1)} %copy.113, bf16[16,128,128]{1,2,0:T(8,128)(2,1)} %copy.112, bf16[16,128,16]{1,2,0:T(8,128)(2,1)S(1)} %copy.111, bf16[1,160,128]{2,0,1:T(2,128)(2,1)S(1)} %get-tuple-element.47), kind=kOutput, calls=%fused_computation.98 | convolution fusion | flops 85852160 | bytes 1744896 | tf_op jit(solution)/shard_map/rnj,jc->rnc/dot_general | solution.py:101
  97.8 2.4 %reshape.184 = f32[16,16,1024]{2,1,0:T(8,128)} reshape(f32[16,128,128]{2,1,0:T(8,128)} %fusion.76) | data formatting | bytes 2097152 | tf_op jit(solution)/shard_map/reshape | solution.py:103
  100.2 13.3 %fusion.23 = bf16[16,16,1024]{2,0,1:T(8,128)(2,1)} fusion(f32[16,16,1024]{2,1,0:T(8,128)} %reshape.184, f32[16,16,1024]{2,1,0:T(8,128)} %reshape.182, f32[16,16,1024]{2,1,0:T(8,128)} %reshape.180, f32[16,16,1024]{2,1,0:T(8,128)} %reshape.178, f32[16,16,1024]{2,1,0:T(8,128)} %reshape.176, f32[16,16,1024]{2,1,0:T(8,128)S(1)} %reshape.174, ...), kind=kLoop, calls=%fused_computation.47 | loop fusion | flops 6291456 | bytes 8912928 | tf_op jit(solution)/shard_map/convert_element_type | solution.py:105
  113.4 11.0 %all-to-all-start = ((bf16[16,16,1024]{2,0,1:T(8,128)(2,1)}), bf16[16,16,1024]{2,0,1:T(8,128)(2,1)S(1)}, u32[]{:S(2)}, u32[]{:S(2)}) async-start(bf16[16,16,1024]{2,0,1:T(8,128)(2,1)} %fusion.23), calls=%async_computation | async-start | bytes 1048576 | tf_op jit(solution)/shard_map/all_to_all | solution.py:107
  124.9 2.6 %iota_subtract_fusion = s32[1024,1080]{0,1:T(8,128)} fusion(), kind=kLoop, calls=%fused_computation.18 | loop fusion | flops 1105920 | bytes 4423680 | tf_op jit(solution)/shard_map/sub | solution.py:41
  127.5 11.2 %all-to-all-done = bf16[16,16,1024]{2,0,1:T(8,128)(2,1)S(1)} async-done(((bf16[16,16,1024]{2,0,1:T(8,128)(2,1)}), bf16[16,16,1024]{2,0,1:T(8,128)(2,1)S(1)}, u32[]{:S(2)}, u32[]{:S(2)}) %all-to-all-start) | async-done | bytes 524320 | tf_op jit(solution)/shard_map/all_to_all | solution.py:107
  140.1 3.0 %collective-permute-start.2 = (bf16[256,28]{1,0:T(8,128)(2,1)S(1)}, bf16[256,28]{1,0:T(8,128)(2,1)S(1)}, u32[]{:S(2)}, u32[]{:S(2)}) collective-permute-start(bf16[256,28]{1,0:T(8,128)(2,1)S(1)} %get-tuple-element.45), channel_id=1, source_target_pairs={{0,1},{1,2},{2,3},{3,4},{4,5},{5,6},{6,7},{7,8},{8,9},{9,10},{10,1... | collective-permute-start | bytes 43016 | tf_op jit(solution)/shard_map/ppermute | solution.py:26
  145.7 10.7 %fusion.12 = f32[2,128,1024]{2,1,0:T(8,128)S(1)} fusion(f32[2]{0:T(128)S(1)} %get-tuple-element.16, f32[2]{0:T(128)S(1)} %get-tuple-element.17, f32[2]{0:T(128)S(1)} %get-tuple-element.18, f32[2]{0:T(128)S(1)} %get-tuple-element.19, f32[2]{0:T(128)S(1)} %get-tuple-element.20, f32[2]{0:T(128)S(1)} %get-tuple-element.21, f32[2]{0:T(128)S(1)} %get-tuple-element.22, ...), kind=kOutput, calls=%fused_computation.33 | convolution fusion | flops 730155776 | bytes 6885784 | tf_op jit(solution)/shard_map/brs,bcs->brc/dot_general | solution.py:63
  157.6 32.8 %all-reduce.10 = (f32[]{:T(128)}, f32[]{:T(128)}) all-reduce(f32[]{:T(128)} %get-tuple-element.6, f32[]{:T(128)} %get-tuple-element.5), channel_id=1, replica_groups=mesh['swath'=2,'band'=16] {'band'}, use_global_device_ids=true, to_apply=%region_3.4 | all-reduce | flops 2 | bytes 16 | tf_op jit(solution)/shard_map/psum | solution.py:118
  (126 shorter events, 51.3 us)
Async XLA Ops:
  0.0 10.2 %copy-start = (bf16[8,33]{1,0:T(8,128)(2,1)S(1)}, bf16[8,33]{1,0:T(8,128)(2,1)}, u32[]{:S(2)}) copy-start(bf16[8,33]{1,0:T(8,128)(2,1)} %param.11) | copy-start | bytes 1588
  0.0 12.1 %collective-permute-start = (bf16[16,16384]{1,0:T(8,128)(2,1)}, bf16[16,16384]{1,0:T(8,128)(2,1)S(1)}, u32[]{:S(2)}, u32[]{:S(2)}) collective-permute-start(bf16[16,16384]{1,0:T(8,128)(2,1)} %param.9), channel_id=1, source_target_pairs={{0,1},{1,2},{2,3},{3,4},{4,5},{5,6},{6,7},{7,8},{8,9},{9,10},{10,1... | collective-permute-start | bytes 1572872 | tf_op jit(solution)/shard_map/ppermute | solution.py:26
  2.6 9.7 %collective-permute-start.1 = (bf16[16,16384]{1,0:T(8,128)(2,1)}, bf16[16,16384]{1,0:T(8,128)(2,1)S(1)}, u32[]{:S(2)}, u32[]{:S(2)}) collective-permute-start(bf16[16,16384]{1,0:T(8,128)(2,1)} %param.9), channel_id=1, source_target_pairs={{1,0},{2,1},{3,2},{4,3},{5,4},{6,5},{7,6},{8,7},{9,8},{10,9},{11,1... | collective-permute-start | bytes 1572872 | tf_op jit(solution)/shard_map/ppermute | solution.py:28
  4.6 5.7 %copy-start.17 = (f32[2]{0:T(128)}, f32[2]{0:T(128)S(1)}, u32[]{:S(2)}) copy-start(f32[2]{0:T(128)S(1)} %convert_bitcast_fusion) | copy-start | bytes 28
  10.2 1.9 %copy-start.8 = (bf16[16,16384]{1,0:T(8,128)(2,1)S(1)}, bf16[16,16384]{1,0:T(8,128)(2,1)}, u32[]{:S(2)}) copy-start(bf16[16,16384]{1,0:T(8,128)(2,1)} %param.9) | copy-start | bytes 1572868
  18.8 1.3 copy-start.10
  32.0 2.2 %copy-start.2 = (bf16[16,128,128]{2,1,0:T(8,128)(2,1)S(1)}, bf16[16,128,128]{2,1,0:T(8,128)(2,1)}, u32[]{:S(2)}) copy-start(bf16[16,128,128]{2,1,0:T(8,128)(2,1)} %slice.311) | copy-start | bytes 1572868
  33.0 1.5 copy-start.7
  33.0 1.7 copy-start.6
  34.2 0.9 copy-start.9
  35.1 3.0 %copy-start.1 = (bf16[16,128,128]{2,1,0:T(8,128)(2,1)S(1)}, bf16[16,128,128]{2,1,0:T(8,128)(2,1)}, u32[]{:S(2)}) copy-start(bf16[16,128,128]{2,1,0:T(8,128)(2,1)} %slice.316) | copy-start | bytes 1572868
  36.6 2.6 %copy-start.5 = (bf16[16,128,16]{2,1,0:T(8,128)(2,1)S(1)}, bf16[16,128,16]{2,1,0:T(8,128)(2,1)}, u32[]{:S(2)}) copy-start(bf16[16,128,16]{2,1,0:T(8,128)(2,1)} %get-tuple-element.30) | copy-start | bytes 196612
  36.6 2.8 %copy-start.4 = (bf16[16,128,16]{2,1,0:T(8,128)(2,1)S(1)}, bf16[16,128,16]{2,1,0:T(8,128)(2,1)}, u32[]{:S(2)}) copy-start(bf16[16,128,16]{2,1,0:T(8,128)(2,1)} %get-tuple-element.31) | copy-start | bytes 196612
  42.1 3.7 %copy-start.3 = (bf16[16,128,16]{2,1,0:T(8,128)(2,1)S(1)}, bf16[16,128,16]{2,1,0:T(8,128)(2,1)}, u32[]{:S(2)}) copy-start(bf16[16,128,16]{2,1,0:T(8,128)(2,1)} %get-tuple-element.33) | copy-start | bytes 196612
  100.2 24.3 %copy-start.14 = (s32[2]{0:T(128)S(1)}, s32[2]{0:T(128)}, u32[]{:S(2)}) copy-start(s32[2]{0:T(128)} %get-tuple-element.64) | copy-start | bytes 28
  100.2 24.3 %copy-start.16 = (bf16[32,8]{0,1:T(8,128)(2,1)S(1)}, bf16[32,8]{0,1:T(8,128)(2,1)}, u32[]{:S(2)}) copy-start(bf16[32,8]{0,1:T(8,128)(2,1)} %param.13) | copy-start | bytes 1540
  100.2 24.5 %copy-start.13 = (s32[2]{0:T(128)S(1)}, s32[2]{0:T(128)}, u32[]{:S(2)}) copy-start(s32[2]{0:T(128)} %get-tuple-element.65) | copy-start | bytes 28
  113.4 25.3 %all-to-all-start = ((bf16[16,16,1024]{2,0,1:T(8,128)(2,1)}), bf16[16,16,1024]{2,0,1:T(8,128)(2,1)S(1)}, u32[]{:S(2)}, u32[]{:S(2)}) async-start(bf16[16,16,1024]{2,0,1:T(8,128)(2,1)} %fusion.23), calls=%async_computation | async-start | bytes 1048576 | tf_op jit(solution)/shard_map/all_to_all | solution.py:107
  138.8 4.8 %collective-permute-start.3 = (bf16[256,28]{1,0:T(8,128)(2,1)S(1)}, bf16[256,28]{1,0:T(8,128)(2,1)S(1)}, u32[]{:S(2)}, u32[]{:S(2)}) collective-permute-start(bf16[256,28]{1,0:T(8,128)(2,1)S(1)} %get-tuple-element.44), channel_id=1, source_target_pairs={{1,0},{2,1},{3,2},{4,3},{5,4},{6,5},{7,6},{8,7},{9,8},{10,9},{11,1... | collective-permute-start | bytes 43016 | tf_op jit(solution)/shard_map/ppermute | solution.py:28
  140.1 3.9 %collective-permute-start.2 = (bf16[256,28]{1,0:T(8,128)(2,1)S(1)}, bf16[256,28]{1,0:T(8,128)(2,1)S(1)}, u32[]{:S(2)}, u32[]{:S(2)}) collective-permute-start(bf16[256,28]{1,0:T(8,128)(2,1)S(1)} %get-tuple-element.45), channel_id=1, source_target_pairs={{0,1},{1,2},{2,3},{3,4},{4,5},{5,6},{6,7},{7,8},{8,9},{9,10},{10,1... | collective-permute-start | bytes 43016 | tf_op jit(solution)/shard_map/ppermute | solution.py:26
  144.6 0.9 copy-start.11
  144.7 0.9 copy-start.12
  144.7 1.0 copy-start.15
  144.7 1.0 copy-start.18
where the time goes:
time: 196 us; the launch traced here: 194 us
  local copies, waits for them, and re-layouts  73.8 us (38%)
  matrix products  34.7 us (18%)
  blocking collectives  32.8 us (17%)
  starting transfers between devices  19.2 us (10%)
  other arithmetic  18.7 us (10%)
  waiting for transfers between devices  11.7 us (6%)
  between operations  3.08 us (2%)
    psum x1, blocking collectives, on_device(): lax.psum((jnp.sum(filtered), jnp.sum(filtered * filtered)), 'band')  32.8 us
    unnamed x64, local copies, waits for them, and re-layouts  30.6 us
    dot_general x8, matrix products, on_device(): jnp.einsum('rnj,jc->rnc', stacked, column_mats[kernel], preferred_element...  19.4 us
    reshape x8, local copies, waits for them, and re-layouts, on_device(): field = jnp.einsum('rnj,jc->rnc', stacked, column_mats[kernel], preferred...  16.2 us
    convert_element_type x1, other arithmetic, on_device(): intensity = total.astype(jnp.bfloat16)  13.3 us
    all_to_all x1, waiting for transfers between devices, on_device(): lax.all_to_all(intensity, 'band', split_axis=1, concat_axis=0, tiled=True)  11.2 us
    all_to_all x1, starting transfers between devices, on_device(): lax.all_to_all(intensity, 'band', split_axis=1, concat_axis=0, tiled=True)  11 us
    dot_general x1, matrix products, warp_strip(): jnp.einsum('brs,bcs->brc', partial_value, column_matrix, preferred_elemen...  10.7 us
  transfers between devices with their start and end apart: 5, of which 2 were waited for; matrix products, arithmetic and copies ran while one was open for 6% of the time, Pallas kernels for 0%

commit v1 on v0

v1 whole, which is shorter than its diff:
```python
import functools

import jax
import jax.numpy as jnp
from jax import lax
from jax.experimental import pallas as pl
from jax.experimental.pallas import tpu as pltpu
from jax.sharding import PartitionSpec as P

BLK = 128
P_SIZE = 28
LANES = 128
WIN = 256
ZERO = 160

epsilon = 1e-05


class Plan:
    def __init__(self, devices, rows_dev, width, kernels, reach, taps):
        self.devices, self.rows_dev, self.width = devices, rows_dev, width
        self.kernels, self.reach, self.taps = kernels, reach, taps
        self.half = reach // 2
        self.height = rows_dev * devices
        self.strip = width // devices
        self.piece = self.strip + LANES
        self.blocks = self.height // BLK
        self.tile_rows = min(self.height, 256)
        self.row_tiles = self.height // self.tile_rows
        self.pad = 0 if self.row_tiles == 1 else LANES
        self.window = self.tile_rows + 2 * self.pad
        self.step = WIN - 2 * self.half
        self.tile_cols = min(self.strip, 256)
        self.col_tiles = self.strip // self.tile_cols
        self.chunks = pl.cdiv(self.strip + 2 * P_SIZE, self.step)
        self.lead = P_SIZE + self.half
        self.pairs = []
        for q in range(self.col_tiles):
            first = (self.tile_cols * q + 1) // self.step
            last = min((self.tile_cols * (q + 1) - 1 + 2 * P_SIZE) // self.step, self.chunks - 1)
            self.pairs += [(q, c) for c in range(first, last + 1)]
        self.ext = pl.cdiv(LANES + self.step * self.chunks + WIN, LANES) * LANES


def send_kernel(plan, design, out):
    lane = lax.broadcasted_iota(jnp.int32, (plan.rows_dev, LANES), 1)
    zero = jnp.zeros((plan.rows_dev, LANES), design.dtype)
    strip = plan.strip
    for s in range(plan.devices):
        at = s * strip
        out[s, :, :strip] = design[:, at : at + strip]
        before = design[:, at - LANES : at] if s else zero
        after = design[:, at + strip : at + strip + LANES] if s < plan.devices - 1 else zero
        out[s, :, strip:] = jnp.where(lane < LANES // 2, after, before)


def matrix_kernel(
    plan, row_taps, column_taps, interp, shift, phase, rows, columns, up, across, tap_rows, tap_cols, fine, fine_back
):
    wide = 3 * LANES
    for held in (tap_rows, tap_cols, fine, fine_back):
        held[...] = jnp.zeros_like(held)
    tap_rows[:, : plan.reach] = row_taps[...].astype(jnp.float32)
    fine[:, : plan.taps] = interp[...].astype(jnp.float32)
    a = lax.broadcasted_iota(jnp.int32, (LANES, LANES), 0)
    b = lax.broadcasted_iota(jnp.int32, (LANES, LANES), 1)

    def flipped(held, count):
        swap = jnp.where(a + b == count - 1, 1.0, 0.0).astype(jnp.bfloat16)
        return jnp.dot(held[:, :LANES].astype(jnp.bfloat16), swap, preferred_element_type=jnp.float32)

    tap_cols[:, : plan.reach] = column_taps[...].astype(jnp.float32)
    tap_cols[:, :LANES] = flipped(tap_cols, plan.reach)
    fine_back[:, :LANES] = flipped(fine, plan.taps)
    zero = jnp.zeros((16, LANES), jnp.bfloat16)
    row = lax.broadcasted_iota(jnp.int32, (16, wide), 0)

    def tiles(taps, moved):
        base = pltpu.roll(jnp.broadcast_to(taps, (16, wide)), ZERO + moved, 1)
        for bit in (1, 2, 4, 8):
            base = jnp.where((row & bit) != 0, pltpu.roll(base, bit, 1), base)
        return {m - ZERO: base[:, m : m + LANES].astype(jnp.bfloat16) for m in range(16, 208, 16)}

    def toeplitz(out, at, bank, offset, count, cols, used=None):
        for g in range(count // 16):
            for j in range(cols // LANES):
                start = LANES * j - 16 * g - offset
                tile = bank.get(start, zero) if used is None or 16 * g < used else zero
                out[pl.ds(pl.multiple_of(at + 16 * g, 16), 16), LANES * j : LANES * (j + 1)] = tile

    def per_kernel(k, carry):
        bank = tiles(tap_rows[pl.ds(k, 1), :], 0)
        toeplitz(rows, k * plan.tile_rows, bank, plan.pad - plan.half, plan.tile_rows, plan.window)
        bank = tiles(tap_cols[pl.ds(k, 1), :], 0)
        toeplitz(columns, k * WIN, bank, 1 - plan.reach, WIN, WIN)
        return carry

    lax.fori_loop(0, plan.kernels, per_kernel, 0)
    middle = plan.taps // 2 - 1
    for b in range(plan.blocks):
        inside = (b * BLK) % plan.tile_rows
        bank = tiles(fine[pl.ds(phase[0, b, 0], 1), :], shift[0, b, 0] - middle)
        toeplitz(up, b * BLK, bank, plan.pad + inside, BLK, plan.window)
        bank = tiles(fine_back[pl.ds(phase[1, b, 0], 1), :], -shift[1, b, 0])
        for at, (q, c) in enumerate(plan.pairs):
            offset = plan.step * c - plan.tile_cols * q - P_SIZE + middle - (plan.taps - 1)
            toeplitz(across, (b * len(plan.pairs) + at) * WIN, bank, offset, WIN, plan.tile_cols, plan.step)


def main_kernel(
    plan, design, rows, columns, up, across, weight, care, image, filtered, sums, ext, chunk, smooth, intensity, partial, diff
):
    high, pad, tile = plan.height, plan.pad, plan.tile_rows
    strip = plan.strip
    place = lax.axis_index("band")
    if pad:
        ext[...] = jnp.zeros_like(ext)
        intensity[...] = jnp.zeros_like(intensity)
    elif plan.ext > strip + 2 * LANES:
        ext[:, strip + 2 * LANES :] = jnp.zeros((high, plan.ext - strip - 2 * LANES), ext.dtype)
    ext[pad : pad + high, :LANES] = design[:, strip:]
    ext[pad : pad + high, LANES : LANES + strip] = design[:, :strip]
    ext[pad : pad + high, LANES + strip : 2 * LANES + strip] = design[:, strip:]
    for c in range(plan.chunks):
        at = LANES - plan.lead + plan.step * c
        chunk[c] = ext[:, at : at + WIN]

    def render(c, carry):
        column = lax.broadcasted_iota(jnp.int32, (tile, WIN), 1) + (plan.step * c - P_SIZE + place * strip)
        inside = (column >= 0) & (column < plan.width)
        for r in range(plan.row_tiles):
            smooth[...] = jnp.dot(
                rows[...], chunk[c, tile * r : tile * r + plan.window, :], preferred_element_type=jnp.float32
            ).astype(jnp.bfloat16)
            total = jnp.zeros((tile, WIN), jnp.float32)
            for k in range(plan.kernels):
                field = jnp.dot(
                    smooth[tile * k : tile * (k + 1), :],
                    columns[WIN * k : WIN * (k + 1), :],
                    preferred_element_type=jnp.float32,
                )
                total = total + weight[k] * field * field
            intensity[c, pad + tile * r : pad + tile * (r + 1), :] = jnp.where(inside, total, 0.0).astype(jnp.bfloat16)
        for r in range(plan.row_tiles):
            partial[c, tile * r : tile * (r + 1), :] = jnp.dot(
                up[tile * r : tile * (r + 1), :],
                intensity[c, tile * r : tile * r + plan.window, :],
                preferred_element_type=jnp.float32,
            ).astype(jnp.bfloat16)
        return carry

    lax.fori_loop(0, plan.chunks, render, 0)

    diff[:8, :] = jnp.zeros((8, strip), jnp.float32)
    diff[8 + high :, :] = jnp.zeros((8, strip), jnp.float32)
    for b in range(plan.blocks):
        cared = care[b, 0].astype(jnp.float32)
        for q in range(plan.col_tiles):
            warped = jnp.zeros((BLK, plan.tile_cols), jnp.float32)
            for at, (tile_at, c) in enumerate(plan.pairs):
                if tile_at == q:
                    start = (b * len(plan.pairs) + at) * WIN
                    warped = warped + jnp.dot(
                        partial[c, BLK * b : BLK * (b + 1), :],
                        across[start : start + WIN, :],
                        preferred_element_type=jnp.float32,
                    )
            cols = slice(plan.tile_cols * q, plan.tile_cols * (q + 1))
            measured = image[BLK * b : BLK * (b + 1), cols].astype(jnp.float32)
            diff[8 + BLK * b : 8 + BLK * (b + 1), cols] = cared * (measured - warped)
    first = jnp.zeros((8, LANES), jnp.float32)
    second = jnp.zeros((8, LANES), jnp.float32)
    for at in range(0, strip, LANES):
        cols = slice(at, at + LANES)
        value = diff[8 : 8 + high, cols] + 0.5 * (diff[7 : 7 + high, cols] + diff[9 : 9 + high, cols])
        filtered[:, cols] = value
        split = value.reshape(high // 8, 8, LANES)
        first = first + jnp.sum(split, axis=0)
        second = second + jnp.sum(split * split, axis=0)
    sums[0] = first
    sums[1] = second


def last_kernel(plan, filtered, sums, care, out):
    cells = plan.height * plan.width
    mean = jnp.sum(sums[0]) / cells
    variance = jnp.sum(sums[1]) / cells - mean * mean
    scale = lax.rsqrt(jnp.full((1, LANES), variance + epsilon, jnp.float32))
    for b in range(plan.blocks):
        cared = care[b, 0].astype(jnp.float32)
        for at in range(0, plan.strip, LANES):
            value = filtered[BLK * b : BLK * (b + 1), at : at + LANES]
            out[BLK * b : BLK * (b + 1), at : at + LANES] = (cared * ((value - mean) * scale)).astype(out.dtype)


VMEM = pl.BlockSpec(memory_space=pltpu.VMEM)
SMEM = pl.BlockSpec(memory_space=pltpu.SMEM)


def total_over(values, axis):
    count = lax.axis_size(axis)
    if count & (count - 1):
        return lax.psum(values, axis)
    bit = 1
    while bit < count:
        values = values + lax.ppermute(values, axis, [(i, i ^ bit) for i in range(count)])
        bit *= 2
    return values


def on_device(
    design, row_taps, column_taps, kernel_weight, interp, block_shift, block_phase, care, image
):
    plan = Plan(
        lax.axis_size("band"), design.shape[0], design.shape[1], row_taps.shape[0], row_taps.shape[1], interp.shape[1]
    )
    bf16, f32 = jnp.bfloat16, jnp.float32
    high, strip, kernels = plan.height, plan.strip, plan.kernels
    send = pl.pallas_call(
        functools.partial(send_kernel, plan),
        out_shape=jax.ShapeDtypeStruct((plan.devices, plan.rows_dev, plan.piece), bf16),
        in_specs=[VMEM],
        out_specs=VMEM,
    )(design)
    got = lax.all_to_all(send, "band", 0, 0, tiled=True).reshape(high, plan.piece)
    rows, columns, up, across = pl.pallas_call(
        functools.partial(matrix_kernel, plan),
        out_shape=[
            jax.ShapeDtypeStruct((kernels * plan.tile_rows, plan.window), bf16),
            jax.ShapeDtypeStruct((kernels * WIN, WIN), bf16),
            jax.ShapeDtypeStruct((high, plan.window), bf16),
            jax.ShapeDtypeStruct((plan.blocks * len(plan.pairs) * WIN, plan.tile_cols), bf16),
        ],
        in_specs=[VMEM, VMEM, VMEM, SMEM, SMEM],
        out_specs=[VMEM] * 4,
        scratch_shapes=[
            pltpu.VMEM((kernels, 3 * LANES), f32),
            pltpu.VMEM((kernels, 3 * LANES), f32),
            pltpu.VMEM((interp.shape[0], 3 * LANES), f32),
            pltpu.VMEM((interp.shape[0], 3 * LANES), f32),
        ],
        cost_estimate=pl.CostEstimate(flops=10**9, bytes_accessed=8 * 10**6, transcendentals=0),
    )(row_taps, column_taps, interp, block_shift, block_phase)
    filtered, sums = pl.pallas_call(
        functools.partial(main_kernel, plan),
        out_shape=[
            jax.ShapeDtypeStruct((high, strip), f32),
            jax.ShapeDtypeStruct((2, 8, LANES), f32),
        ],
        in_specs=[VMEM] * 5 + [SMEM, SMEM, VMEM],
        out_specs=[VMEM] * 2,
        scratch_shapes=[
            pltpu.VMEM((high + 2 * plan.pad, plan.ext), bf16),
            pltpu.VMEM((plan.chunks, high + 2 * plan.pad, WIN), bf16),
            pltpu.VMEM((kernels * plan.tile_rows, WIN), bf16),
            pltpu.VMEM((plan.chunks, high + 2 * plan.pad, WIN), bf16),
            pltpu.VMEM((plan.chunks, high, WIN), bf16),
            pltpu.VMEM((high + 16, strip), f32),
        ],
        cost_estimate=pl.CostEstimate(flops=4 * 10**9, bytes_accessed=8 * 10**6, transcendentals=0),
    )(got, rows, columns, up, across, kernel_weight, care, image)
    sums = total_over(sums, "band")
    return pl.pallas_call(
        functools.partial(last_kernel, plan),
        out_shape=jax.ShapeDtypeStruct((high, strip), bf16),
        in_specs=[VMEM, VMEM, SMEM],
        out_specs=VMEM,
    )(filtered, sums, care)


def solution(mesh):
    placed = (
        P(("swath", "band"), None),
        P(),
        P(),
        P(),
        P(),
        P(None, "swath", "band"),
        P(None, "swath", "band"),
        P("swath", "band"),
        P("swath", "band"),
    )
    return jax.shard_map(
        on_device, mesh=mesh, in_specs=placed, out_specs=P("swath", "band"), check_vma=False
    )
```

time: 196 us -> 52.5 us (0.27)
  local copies, waits for them, and re-layouts: 73.8 us -> 3.58 us
  matrix products: 34.7 us -> 0 us
  blocking collectives: 32.8 us -> 0 us
  Pallas kernels: 0 us -> 21.1 us
  other arithmetic: 18.7 us -> 1.3 us
  starting transfers between devices: 19.2 us -> 13.5 us
  between operations: 3.08 us -> 0.03 us
    dot_general x21 -> x0, matrix products: 34.7 us -> none  [the longest x8 19.4 us: on_device(): jnp.einsum('rnj,jc->rnc', stacked, column_mats[kernel], preferred_element...]
    psum x1 -> x0, blocking collectives: 32.8 us -> none  [on_device(): lax.psum((jnp.sum(filtered), jnp.sum(filtered * filtered)), 'band')]
    unnamed x64 -> x14, local copies, waits for them, and re-layouts: 30.6 us -> 3.58 us
    pallas_call x0 -> x4, Pallas kernels: none -> 21.1 us  [the longest x1 9.6 us: on_device(): pl.pallas_call(functools.partial(main_kernel, plan), out_shape=[jax.Shape...]
    slice x24 -> x0, local copies, waits for them, and re-layouts: 20.8 us -> none  [the longest x8 9.68 us: on_device(): framed[:, :-2, panel - KH:]]
    reshape x16 -> x0, local copies, waits for them, and re-layouts: 18.2 us -> none  [the longest x8 16.2 us: on_device(): field = jnp.einsum('rnj,jc->rnc', stacked, column_mats[kernel], preferred...]
    convert_element_type x3 -> x0, other arithmetic: 14.9 us -> none  [the longest x1 13.3 us: on_device(): intensity = total.astype(jnp.bfloat16)]
    ppermute x4, waiting for transfers between devices: 0.45 us -> 7.17 us  [total_over(): lax.ppermute(values, axis, [(i, i ^ bit) for i in range(count)])]
  transfers between devices with their start and end apart: 5 -> 5, of which waited for: 2 -> 5; matrix products, arithmetic and copies ran while one was open for 6% -> 5% of each run, Pallas kernels for 0% -> 14%
where the time goes in v1:
time: 52.5 us; the launch traced here: 52.1 us
  Pallas kernels  21.1 us (40%)
  starting transfers between devices  13.5 us (26%)
  waiting for transfers between devices  12.7 us (24%)
  local copies, waits for them, and re-layouts  3.58 us (7%)
  other arithmetic  1.3 us (2%)
    pallas_call x1, Pallas kernels, on_device(): pl.pallas_call(functools.partial(main_kernel, plan), out_shape=[jax.Shape...  9.6 us
    all_to_all x1, starting transfers between devices, on_device(): lax.all_to_all(send, 'band', 0, 0, tiled=True).reshape(high, plan.piece)  7.41 us
    ppermute x4, waiting for transfers between devices, total_over(): lax.ppermute(values, axis, [(i, i ^ bit) for i in range(count)])  7.17 us
    pallas_call x1, Pallas kernels, on_device(): pl.pallas_call(functools.partial(matrix_kernel, plan), out_shape=[jax.Sha...  7.14 us
    ppermute x4, starting transfers between devices, total_over(): lax.ppermute(values, axis, [(i, i ^ bit) for i in range(count)])  6.07 us
    all_to_all x1, waiting for transfers between devices, on_device(): lax.all_to_all(send, 'band', 0, 0, tiled=True).reshape(high, plan.piece)  5.5 us
    unnamed x14, local copies, waits for them, and re-layouts  3.58 us
    pallas_call x1, Pallas kernels, on_device(): pl.pallas_call(functools.partial(last_kernel, plan), out_shape=jax.ShapeD...  2.35 us
  transfers between devices with their start and end apart: 5, of which 5 were waited for; matrix products, arithmetic and copies ran while one was open for 5% of the time, Pallas kernels for 14%

profile of v1, /device:TPU:0, one launch (start us, length us, event | category | flops | bytes accessed | tf_op | source)
XLA Modules:
  0.0 52.1 jit_solution(13934776652160914071)
XLA Ops:
  0.0 0.0 copy-start.4
  0.0 0.0 copy-start.2
  0.0 0.0 copy-start.3
  0.0 0.0 copy-start.1
  0.0 2.0 %shard_map.91 = bf16[16,16,1152]{2,1,0:T(8,128)(2,1)} custom-call(bf16[16,16384]{1,0:T(8,128)(2,1)} %design.1), custom_call_target="tpu_custom_call" | custom-call | tf_op jit(solution)/shard_map/pallas_call | solution.py:219
  2.0 7.4 %all-to-all-start = ((bf16[16,16,1152]{2,1,0:T(8,128)(2,1)}), bf16[16,16,1152]{2,1,0:T(8,128)(2,1)S(1)}, u32[]{:S(2)}, u32[]{:S(2)}) async-start(bf16[16,16,1152]{2,1,0:T(8,128)(2,1)} %shard_map.91), calls=%async_computation | async-start | bytes 1179648 | tf_op jit(solution)/shard_map/all_to_all | solution.py:225
  9.4 0.0 copy-done.4
  9.4 0.7 %copy.13.care = s32[2,1]{1,0:T(2,128)} copy(s32[2,1]{0,1:T(1,128)S(1)} %copy-done.4) | data formatting | bytes 16 | tf_op args[7]
  10.1 0.0 copy-done.2
  10.1 0.7 %copy.11.shift = s32[2,2,1]{2,1,0:T(2,128)} copy(s32[2,2,1]{1,2,0:T(1,128)S(1)} %copy-done.2) | data formatting | bytes 32 | tf_op args[5]
  10.8 0.0 copy-done.3
  10.8 0.7 %copy.12.phase = s32[2,2,1]{2,1,0:T(2,128)} copy(s32[2,2,1]{1,2,0:T(1,128)S(1)} %copy-done.3) | data formatting | bytes 32 | tf_op args[6]
  11.5 0.0 copy-done.1
  11.5 0.7 %copy.10.interp = bf16[32,8]{1,0:T(8,128)(2,1)} copy(bf16[32,8]{0,1:T(8,128)(2,1)S(1)} %copy-done.1) | data formatting | bytes 1024 | tf_op args[4]
  12.1 7.1 %shard_map.92 = (bf16[2048,256]{1,0:T(8,128)(2,1)}, bf16[2048,256]{1,0:T(8,128)(2,1)}, bf16[256,256]{1,0:T(8,128)(2,1)}, bf16[4096,256]{1,0:T(8,128)(2,1)}) custom-call(bf16[8,33]{1,0:T(8,128)(2,1)} %row_taps.1, bf16[8,33]{1,0:T(8,128)(2,1)} %column_taps.1, bf16[32,8]{1,0:T(8,128)(2,1)} %copy.10.interp, s32[2,2,1]{2,1,0:T(2,128)} %copy.11.shift, ...), custom_call_target="tpu_custom_call" | custom-call | flops 1000000000 | bytes 8000000 | tf_op jit(solution)/shard_map/pallas_call | solution.py:226
  19.3 5.5 %all-to-all-done = bf16[16,16,1152]{2,1,0:T(8,128)(2,1)S(1)} async-done(((bf16[16,16,1152]{2,1,0:T(8,128)(2,1)}), bf16[16,16,1152]{2,1,0:T(8,128)(2,1)S(1)}, u32[]{:S(2)}, u32[]{:S(2)}) %all-to-all-start) | async-done | bytes 589856 | tf_op jit(solution)/shard_map/all_to_all | solution.py:225
  24.8 0.0 copy-start
  24.8 0.8 %copy-done = bf16[16,16,1152]{2,1,0:T(8,128)(2,1)} copy-done((bf16[16,16,1152]{2,1,0:T(8,128)(2,1)}, bf16[16,16,1152]{2,1,0:T(8,128)(2,1)S(1)}, u32[]{:S(2)}) %copy-start) | copy-done | bytes 589848
  25.6 9.6 %shard_map.93 = (f32[256,1024]{1,0:T(8,128)}, f32[2,8,128]{2,1,0:T(8,128)}) custom-call(bf16[256,1152]{1,0:T(8,128)(2,1)} %bitcast.1, bf16[2048,256]{1,0:T(8,128)(2,1)} %get-tuple-element.11.rows, bf16[2048,256]{1,0:T(8,128)(2,1)} %get-tuple-element.12.columns, bf16[256,256]{1,0:T(8,128)(2,1)} %get-tuple-element.13.up, ...), custom_call_target="tpu_custom_call" | custom-call | flops 4000000000 | bytes 8000000 | tf_op jit(solution)/shard_map/pallas_call | solution.py:244
  35.2 0.2 collective-permute-start
  35.5 1.2 %collective-permute-done = f32[2,8,128]{2,1,0:T(8,128)S(1)} collective-permute-done((f32[2,8,128]{2,1,0:T(8,128)}, f32[2,8,128]{2,1,0:T(8,128)S(1)}, u32[]{:S(2)}, u32[]{:S(2)}) %collective-permute-start) | collective-permute-done | bytes 8224 | tf_op jit(solution)/shard_map/ppermute | solution.py:206
  36.6 0.7 %add.12 = f32[2,8,128]{2,1,0:T(8,128)S(1)} add(f32[2,8,128]{2,1,0:T(8,128)} %get-tuple-element.16, f32[2,8,128]{2,1,0:T(8,128)S(1)} %collective-permute-done) | non-fusion elementwise | flops 2048 | bytes 24576 | tf_op jit(solution)/shard_map/add | solution.py:206
  37.3 1.2 %collective-permute-start.1 = (f32[2,8,128]{2,1,0:T(8,128)S(1)}, f32[2,8,128]{2,1,0:T(8,128)S(1)}, u32[]{:S(2)}, u32[]{:S(2)}) collective-permute-start(f32[2,8,128]{2,1,0:T(8,128)S(1)} %add.12), channel_id=1, source_target_pairs={{0,2},{1,3},{2,0},{3,1},{4,6},{5,7},{6,4},{7,5},{8,10},{9,11},{10,... | collective-permute-start | bytes 24584 | tf_op jit(solution)/shard_map/ppermute | solution.py:206
  38.5 2.4 %collective-permute-done.1 = f32[2,8,128]{2,1,0:T(8,128)S(1)} collective-permute-done((f32[2,8,128]{2,1,0:T(8,128)S(1)}, f32[2,8,128]{2,1,0:T(8,128)S(1)}, u32[]{:S(2)}, u32[]{:S(2)}) %collective-permute-start.1) | collective-permute-done | bytes 8224 | tf_op jit(solution)/shard_map/ppermute | solution.py:206
  41.0 1.9 %collective-permute-start.2 = (f32[2,8,128]{2,1,0:T(8,128)S(1)}, f32[2,8,128]{2,1,0:T(8,128)S(1)}, u32[]{:S(2)}, u32[]{:S(2)}) collective-permute-start(f32[2,8,128]{2,1,0:T(8,128)S(1)} %add.13), channel_id=1, source_target_pairs={{0,4},{1,5},{2,6},{3,7},{4,0},{5,1},{6,2},{7,3},{8,12},{9,13},{10,... | collective-permute-start | bytes 24584 | tf_op jit(solution)/shard_map/ppermute | solution.py:206
  42.8 1.8 %collective-permute-done.2 = f32[2,8,128]{2,1,0:T(8,128)S(1)} collective-permute-done((f32[2,8,128]{2,1,0:T(8,128)S(1)}, f32[2,8,128]{2,1,0:T(8,128)S(1)}, u32[]{:S(2)}, u32[]{:S(2)}) %collective-permute-start.2) | collective-permute-done | bytes 8224 | tf_op jit(solution)/shard_map/ppermute | solution.py:206
  44.6 2.7 %collective-permute-start.3 = (f32[2,8,128]{2,1,0:T(8,128)S(1)}, f32[2,8,128]{2,1,0:T(8,128)S(1)}, u32[]{:S(2)}, u32[]{:S(2)}) collective-permute-start(f32[2,8,128]{2,1,0:T(8,128)S(1)} %add.14), channel_id=1, source_target_pairs={{0,8},{1,9},{2,10},{3,11},{4,12},{5,13},{6,14},{7,15},{8,0},{9,1},... | collective-permute-start | bytes 24584 | tf_op jit(solution)/shard_map/ppermute | solution.py:206
  47.3 1.8 %collective-permute-done.3 = f32[2,8,128]{2,1,0:T(8,128)S(1)} collective-permute-done((f32[2,8,128]{2,1,0:T(8,128)S(1)}, f32[2,8,128]{2,1,0:T(8,128)S(1)}, u32[]{:S(2)}, u32[]{:S(2)}) %collective-permute-start.3) | collective-permute-done | bytes 8224 | tf_op jit(solution)/shard_map/ppermute | solution.py:206
  49.2 0.6 %add.15.sums = f32[2,8,128]{2,1,0:T(8,128)} add(f32[2,8,128]{2,1,0:T(8,128)S(1)} %add.14, f32[2,8,128]{2,1,0:T(8,128)S(1)} %collective-permute-done.3) | non-fusion elementwise | flops 2048 | bytes 24576 | tf_op jit(solution)/shard_map/add | solution.py:206
  49.8 2.3 %shard_map.94 = bf16[256,1024]{1,0:T(8,128)(2,1)} custom-call(f32[256,1024]{1,0:T(8,128)} %get-tuple-element.15.filtered, f32[2,8,128]{2,1,0:T(8,128)} %add.15.sums, s32[2,1]{1,0:T(2,128)} %copy.13.care), custom_call_target="tpu_custom_call" | custom-call | tf_op jit(solution)/shard_map/pallas_call | solution.py:263
  (2 shorter events, 0.0 us)
Async XLA Ops:
  0.0 9.4 %copy-start.4 = (s32[2,1]{0,1:T(1,128)S(1)}, s32[2,1]{0,1:T(1,128)}, u32[]{:S(2)}) copy-start(s32[2,1]{0,1:T(1,128)} %param.16) | copy-start | bytes 28
  0.0 10.1 %copy-start.2 = (s32[2,2,1]{1,2,0:T(1,128)S(1)}, s32[2,2,1]{1,2,0:T(1,128)}, u32[]{:S(2)}) copy-start(s32[2,2,1]{1,2,0:T(1,128)} %param.14) | copy-start | bytes 52
  0.0 10.8 %copy-start.3 = (s32[2,2,1]{1,2,0:T(1,128)S(1)}, s32[2,2,1]{1,2,0:T(1,128)}, u32[]{:S(2)}) copy-start(s32[2,2,1]{1,2,0:T(1,128)} %param.15) | copy-start | bytes 52
  0.0 11.5 %copy-start.1 = (bf16[32,8]{0,1:T(8,128)(2,1)S(1)}, bf16[32,8]{0,1:T(8,128)(2,1)}, u32[]{:S(2)}) copy-start(bf16[32,8]{0,1:T(8,128)(2,1)} %param.13) | copy-start | bytes 1540
  2.0 22.8 %all-to-all-start = ((bf16[16,16,1152]{2,1,0:T(8,128)(2,1)}), bf16[16,16,1152]{2,1,0:T(8,128)(2,1)S(1)}, u32[]{:S(2)}, u32[]{:S(2)}) async-start(bf16[16,16,1152]{2,1,0:T(8,128)(2,1)} %shard_map.91), calls=%async_computation | async-start | bytes 1179648 | tf_op jit(solution)/shard_map/all_to_all | solution.py:225
  24.8 0.8 %copy-start = (bf16[16,16,1152]{2,1,0:T(8,128)(2,1)}, bf16[16,16,1152]{2,1,0:T(8,128)(2,1)S(1)}, u32[]{:S(2)}) copy-start(bf16[16,16,1152]{2,1,0:T(8,128)(2,1)S(1)} %all-to-all-done) | copy-start | bytes 1769476
  35.2 1.4 %collective-permute-start = (f32[2,8,128]{2,1,0:T(8,128)}, f32[2,8,128]{2,1,0:T(8,128)S(1)}, u32[]{:S(2)}, u32[]{:S(2)}) collective-permute-start(f32[2,8,128]{2,1,0:T(8,128)} %get-tuple-element.16), channel_id=1, source_target_pairs={{0,1},{1,0},{2,3},{3,2},{4,5},{5,4},{6,7},{7,6},{8,9},{9,8},{10,11... | collective-permute-start | bytes 24584 | tf_op jit(solution)/shard_map/ppermute | solution.py:206
  37.3 3.7 %collective-permute-start.1 = (f32[2,8,128]{2,1,0:T(8,128)S(1)}, f32[2,8,128]{2,1,0:T(8,128)S(1)}, u32[]{:S(2)}, u32[]{:S(2)}) collective-permute-start(f32[2,8,128]{2,1,0:T(8,128)S(1)} %add.12), channel_id=1, source_target_pairs={{0,2},{1,3},{2,0},{3,1},{4,6},{5,7},{6,4},{7,5},{8,10},{9,11},{10,... | collective-permute-start | bytes 24584 | tf_op jit(solution)/shard_map/ppermute | solution.py:206
  41.0 3.7 %collective-permute-start.2 = (f32[2,8,128]{2,1,0:T(8,128)S(1)}, f32[2,8,128]{2,1,0:T(8,128)S(1)}, u32[]{:S(2)}, u32[]{:S(2)}) collective-permute-start(f32[2,8,128]{2,1,0:T(8,128)S(1)} %add.13), channel_id=1, source_target_pairs={{0,4},{1,5},{2,6},{3,7},{4,0},{5,1},{6,2},{7,3},{8,12},{9,13},{10,... | collective-permute-start | bytes 24584 | tf_op jit(solution)/shard_map/ppermute | solution.py:206
  44.6 4.5 %collective-permute-start.3 = (f32[2,8,128]{2,1,0:T(8,128)S(1)}, f32[2,8,128]{2,1,0:T(8,128)S(1)}, u32[]{:S(2)}, u32[]{:S(2)}) collective-permute-start(f32[2,8,128]{2,1,0:T(8,128)S(1)} %add.14), channel_id=1, source_target_pairs={{0,8},{1,9},{2,10},{3,11},{4,12},{5,13},{6,14},{7,15},{8,0},{9,1},... | collective-permute-start | bytes 24584 | tf_op jit(solution)/shard_map/ppermute | solution.py:206

commit v2 on v1

v2 whole, which is shorter than its diff:
```python
import functools

import jax
import jax.numpy as jnp
from jax import lax
from jax.experimental import pallas as pl
from jax.experimental.pallas import tpu as pltpu
from jax.sharding import PartitionSpec as P

BLK = 128
P_SIZE = 28
LANES = 128
WIN = 256
ZERO = 160
TILES = 12

epsilon = 1e-05


class Plan:
    def __init__(self, devices, rows_dev, width, kernels, reach, taps):
        self.devices, self.rows_dev, self.width = devices, rows_dev, width
        self.kernels, self.reach, self.taps = kernels, reach, taps
        self.half = reach // 2
        self.height = rows_dev * devices
        self.strip = width // devices
        self.piece = self.strip + LANES
        self.blocks = self.height // BLK
        self.tile_rows = min(self.height, 256)
        self.row_tiles = self.height // self.tile_rows
        self.pad = 0 if self.row_tiles == 1 else LANES
        self.window = self.tile_rows + 2 * self.pad
        self.step = WIN - 2 * self.half
        self.tile_cols = min(self.strip, 256)
        self.col_tiles = self.strip // self.tile_cols
        self.chunks = pl.cdiv(self.strip + 2 * P_SIZE, self.step)
        self.lead = P_SIZE + self.half
        self.pairs = []
        for q in range(self.col_tiles):
            first = (self.tile_cols * q + 1) // self.step
            last = min((self.tile_cols * (q + 1) - 1 + 2 * P_SIZE) // self.step, self.chunks - 1)
            self.pairs += [(q, c) for c in range(first, last + 1)]
        self.parts = 4 if devices % 4 == 0 else 1
        self.ext = pl.cdiv(LANES + self.step * self.chunks + WIN, LANES) * LANES


def send_kernel(plan, design, out, held, arrived):
    lane = lax.broadcasted_iota(jnp.int32, (plan.rows_dev, LANES), 1)
    zero = jnp.zeros((plan.rows_dev, LANES), out.dtype)
    strip, part = plan.strip, plan.width // plan.parts
    copies = [
        pltpu.make_async_copy(design.at[:, pl.ds(i * part, part)], held.at[:, pl.ds(i * part, part)], arrived.at[i])
        for i in range(plan.parts)
    ]
    for copy in copies:
        copy.start()
    for i in range(plan.parts):
        copies[i].wait()
        each = plan.devices // plan.parts
        for s in range(i * each, (i + 1) * each):
            out[s, :, :strip] = held[:, s * strip : (s + 1) * strip]
        for s in range(max(i * each - 1, 0), plan.devices if i == plan.parts - 1 else (i + 1) * each - 1):
            at = s * strip
            before = held[:, at - LANES : at] if s else zero
            after = held[:, at + strip : at + strip + LANES] if s < plan.devices - 1 else zero
            out[s, :, strip:] = jnp.where(lane < LANES // 2, after, before)


def bank_kernel(plan, row_taps, column_taps, interp, shift, phase, rows, columns, up, across, tap_rows, tap_cols, fine, fine_back):
    wide = 3 * LANES
    for held in (tap_rows, tap_cols, fine, fine_back):
        held[...] = jnp.zeros_like(held)
    tap_rows[:, : plan.reach] = row_taps[...].astype(jnp.float32)
    tap_cols[:, : plan.reach] = column_taps[...].astype(jnp.float32)

    def pick(values, side, total=None):
        count = values.shape[side]
        a = lax.broadcasted_iota(jnp.int32, (count, LANES), 0)
        b = lax.broadcasted_iota(jnp.int32, (count, LANES), 1)
        chosen = jnp.where(a == (b if total is None else total - b), 1.0, 0.0).astype(jnp.bfloat16)
        return lax.dot_general(
            values.astype(jnp.bfloat16), chosen, (((side,), (0,)), ((), ())), preferred_element_type=jnp.float32
        )

    tap_cols[:, :LANES] = pick(tap_cols[:, :LANES], 1, plan.reach - 1)
    fine[:, :LANES] = pick(interp[...], 0)
    fine_back[:, :LANES] = pick(interp[...], 0, plan.taps - 1)
    row = lax.broadcasted_iota(jnp.int32, (16, wide), 0)

    def fill(bank, at, taps, moved):
        base = pltpu.roll(jnp.broadcast_to(taps, (16, wide)), ZERO + moved, 1)
        for bit in (1, 2, 4, 8):
            base = jnp.where((row & bit) != 0, pltpu.roll(base, bit, 1), base)
        for m in range(TILES):
            bank[at, 16 * m : 16 * (m + 1), :] = base[:, 16 * (m + 1) : 16 * (m + 1) + LANES].astype(jnp.bfloat16)

    def per_kernel(k, carry):
        fill(rows, k, tap_rows[pl.ds(k, 1), :], 0)
        fill(columns, k, tap_cols[pl.ds(k, 1), :], 0)
        return carry

    lax.fori_loop(0, plan.kernels, per_kernel, 0)
    middle = plan.taps // 2 - 1
    for b in range(plan.blocks):
        fill(up, b, fine[pl.ds(phase[0, 0, b], 1), :], shift[0, 0, b] - middle)
        fill(across, b, fine_back[pl.ds(phase[1, 0, b], 1), :], -shift[1, 0, b])


def band(bank, at, offset, count, cols, used=None):
    assert offset % 16 == 0
    zero = jnp.zeros((16, LANES), jnp.bfloat16)
    tiles = []
    for g in range(count // 16):
        line = []
        for j in range(cols // LANES):
            slot = (LANES * j - 16 * g - offset + ZERO) // 16 - 1
            inside = 0 <= slot < TILES and (used is None or 16 * g < used)
            line.append(bank[at, 16 * slot : 16 * (slot + 1), :] if inside else zero)
        tiles.append(jnp.concatenate(line, axis=1))
    return jnp.concatenate(tiles, axis=0)


def main_kernel(
    plan, design, rows, columns, up, across, weight, care, image, filtered, sums, ext, chunk, intensity, partial, diff
):
    high, pad, tile = plan.height, plan.pad, plan.tile_rows
    strip = plan.strip
    bf16, f32 = jnp.bfloat16, jnp.float32
    place = lax.axis_index("band")
    if pad:
        ext[...] = jnp.zeros_like(ext)
        intensity[...] = jnp.zeros_like(intensity)
    elif plan.ext > strip + 2 * LANES:
        ext[:, strip + 2 * LANES :] = jnp.zeros((high, plan.ext - strip - 2 * LANES), ext.dtype)
    ext[pad : pad + high, :LANES] = design[:, strip:]
    ext[pad : pad + high, LANES : LANES + strip] = design[:, :strip]
    ext[pad : pad + high, LANES + strip : 2 * LANES + strip] = design[:, strip:]
    for c in range(plan.chunks):
        at = LANES - plan.lead + plan.step * c
        chunk[c] = ext[:, at : at + WIN]

    for c in range(plan.chunks):
        column = lax.broadcasted_iota(jnp.int32, (tile, WIN), 1) + (plan.step * c - P_SIZE + place * strip)
        inside = (column >= 0) & (column < plan.width)
        for r in range(plan.row_tiles):
            total = jnp.zeros((tile, WIN), f32)
            for k in range(plan.kernels):
                smooth = jnp.dot(
                    band(rows, k, pad - plan.half, tile, plan.window),
                    chunk[c, tile * r : tile * r + plan.window, :],
                    preferred_element_type=f32,
                ).astype(bf16)
                field = jnp.dot(smooth, band(columns, k, 1 - plan.reach, WIN, WIN), preferred_element_type=f32)
                total = total + weight[k] * field * field
            intensity[c, pad + tile * r : pad + tile * (r + 1), :] = jnp.where(inside, total, 0.0).astype(bf16)
    for c in range(plan.chunks):
        for b in range(plan.blocks):
            at = b * BLK // tile * tile
            partial[c, BLK * b : BLK * (b + 1), :] = jnp.dot(
                band(up, b, pad + b * BLK - at, BLK, plan.window),
                intensity[c, at : at + plan.window, :],
                preferred_element_type=f32,
            ).astype(bf16)

    diff[:8, :] = jnp.zeros((8, strip), f32)
    diff[8 + high :, :] = jnp.zeros((8, strip), f32)
    middle = plan.taps // 2 - 1
    for b in range(plan.blocks):
        cared = care[0, b].astype(f32)
        for q in range(plan.col_tiles):
            warped = jnp.zeros((BLK, plan.tile_cols), f32)
            for tile_at, c in plan.pairs:
                if tile_at == q:
                    offset = plan.step * c - plan.tile_cols * q - P_SIZE + middle - (plan.taps - 1)
                    warped = warped + jnp.dot(
                        partial[c, BLK * b : BLK * (b + 1), :],
                        band(across, b, offset, WIN, plan.tile_cols, plan.step),
                        preferred_element_type=f32,
                    )
            cols = slice(plan.tile_cols * q, plan.tile_cols * (q + 1))
            measured = image[BLK * b : BLK * (b + 1), cols].astype(f32)
            diff[8 + BLK * b : 8 + BLK * (b + 1), cols] = cared * (measured - warped)
    first = jnp.zeros((8, LANES), f32)
    second = jnp.zeros((8, LANES), f32)
    for at in range(0, strip, LANES):
        cols = slice(at, at + LANES)
        value = diff[8 : 8 + high, cols] + 0.5 * (diff[7 : 7 + high, cols] + diff[9 : 9 + high, cols])
        filtered[:, cols] = value
        split = value.reshape(high // 8, 8, LANES)
        first = first + jnp.sum(split, axis=0)
        second = second + jnp.sum(split * split, axis=0)
    both = jnp.concatenate([jnp.sum(first, 0, keepdims=True), jnp.sum(second, 0, keepdims=True)], axis=0)
    for s in range(plan.devices):
        sums[s] = both


def last_kernel(plan, filtered, sums, care, out):
    cells = plan.height * plan.width
    both = jnp.sum(sums[...], axis=0)
    mean = jnp.sum(both[0:1, :]) / cells
    variance = jnp.sum(both[1:2, :]) / cells - mean * mean
    scale = lax.rsqrt(jnp.full((1, LANES), variance + epsilon, jnp.float32))
    for b in range(plan.blocks):
        cared = care[0, b].astype(jnp.float32)
        for at in range(0, plan.strip, LANES):
            value = filtered[BLK * b : BLK * (b + 1), at : at + LANES]
            out[BLK * b : BLK * (b + 1), at : at + LANES] = (cared * ((value - mean) * scale)).astype(out.dtype)


VMEM = pl.BlockSpec(memory_space=pltpu.VMEM)
SMEM = pl.BlockSpec(memory_space=pltpu.SMEM)
FAR = pl.BlockSpec(memory_space=pl.ANY)
GRANT = pltpu.CompilerParams(vmem_limit_bytes=24 << 20)


def near(value):
    return pltpu.with_memory_space_constraint(value, pltpu.VMEM)


def far(value):
    return pltpu.with_memory_space_constraint(value, pltpu.HBM)


def on_device(
    design, row_taps, column_taps, kernel_weight, interp, block_shift, block_phase, care, image
):
    plan = Plan(
        lax.axis_size("band"), design.shape[0], design.shape[1], row_taps.shape[0], row_taps.shape[1], interp.shape[1]
    )
    bf16, f32 = jnp.bfloat16, jnp.float32
    high, strip, kernels = plan.height, plan.strip, plan.kernels
    send = pl.pallas_call(
        functools.partial(send_kernel, plan),
        out_shape=pltpu.VMEM((plan.devices, plan.rows_dev, plan.piece), bf16),
        in_specs=[FAR],
        out_specs=VMEM,
        scratch_shapes=[pltpu.VMEM(design.shape, bf16), pltpu.SemaphoreType.DMA((plan.parts,))],
        compiler_params=GRANT,
    )(far(design))
    got = lax.all_to_all(send, "band", 0, 0, tiled=True).reshape(high, plan.piece)
    bank = lambda count: pltpu.VMEM((count, 16 * TILES, LANES), bf16)
    taps = lambda count: pltpu.VMEM((count, 3 * LANES), f32)
    rows, columns, up, across = pl.pallas_call(
        functools.partial(bank_kernel, plan),
        out_shape=[bank(kernels), bank(kernels), bank(plan.blocks), bank(plan.blocks)],
        in_specs=[VMEM, VMEM, VMEM, SMEM, SMEM],
        out_specs=[VMEM] * 4,
        scratch_shapes=[taps(kernels), taps(kernels), taps(interp.shape[0]), taps(interp.shape[0])],
        compiler_params=GRANT,
        cost_estimate=pl.CostEstimate(flops=10**9, bytes_accessed=8 * 10**6, transcendentals=0),
    )(row_taps, column_taps, interp.T, jnp.swapaxes(block_shift, 1, 2), jnp.swapaxes(block_phase, 1, 2))
    filtered, sums = pl.pallas_call(
        functools.partial(main_kernel, plan),
        out_shape=[pltpu.VMEM((high, strip), f32), pltpu.VMEM((plan.devices, 2, LANES), f32)],
        in_specs=[VMEM] * 5 + [SMEM, SMEM, VMEM],
        out_specs=[VMEM] * 2,
        scratch_shapes=[
            pltpu.VMEM((high + 2 * plan.pad, plan.ext), bf16),
            pltpu.VMEM((plan.chunks, high + 2 * plan.pad, WIN), bf16),
            pltpu.VMEM((plan.chunks, high + 2 * plan.pad, WIN), bf16),
            pltpu.VMEM((plan.chunks, high, WIN), bf16),
            pltpu.VMEM((high + 16, strip), f32),
        ],
        compiler_params=GRANT,
        cost_estimate=pl.CostEstimate(flops=4 * 10**9, bytes_accessed=8 * 10**6, transcendentals=0),
    )(near(got), near(rows), near(columns), near(up), near(across), kernel_weight, care.T, near(image))
    sums = lax.all_to_all(sums, "band", 0, 0, tiled=True)
    return pl.pallas_call(
        functools.partial(last_kernel, plan),
        out_shape=jax.ShapeDtypeStruct((high, strip), bf16),
        in_specs=[VMEM, VMEM, SMEM],
        out_specs=VMEM,
        compiler_params=GRANT,
    )(near(filtered), near(sums), care.T)


def solution(mesh):
    placed = (
        P(("swath", "band"), None),
        P(),
        P(),
        P(),
        P(),
        P(None, "swath", "band"),
        P(None, "swath", "band"),
        P("swath", "band"),
        P("swath", "band"),
    )
    return jax.shard_map(
        on_device, mesh=mesh, in_specs=placed, out_specs=P("swath", "band"), check_vma=False
    )
```

time: 52.5 us -> 42.8 us (0.82)
  blocking collectives: 0 us -> 10.8 us
  Pallas kernels: 21.1 us -> 13.1 us
  starting transfers between devices: 13.5 us -> 7.56 us
  waiting for transfers between devices: 12.7 us -> 9.61 us
  local copies, waits for them, and re-layouts: 3.58 us -> 1.34 us
  other arithmetic: 1.3 us -> 0 us
    all_to_all x0 -> x1, blocking collectives: none -> 10.8 us  [on_device(): sums = lax.all_to_all(sums, 'band', 0, 0, tiled=True)]
    pallas_call x3, Pallas kernels: 18.7 us -> 11.5 us  [the longest x1 5.06 us: on_device(): pl.pallas_call(functools.partial(bank_kernel, plan), out_shape=[bank(kern...]
    ppermute x4 -> x0, waiting for transfers between devices: 7.17 us -> none  [total_over(): lax.ppermute(values, axis, [(i, i ^ bit) for i in range(count)])]
    ppermute x4 -> x0, starting transfers between devices: 6.07 us -> none  [total_over(): lax.ppermute(values, axis, [(i, i ^ bit) for i in range(count)])]
    all_to_all x1, waiting for transfers between devices: 5.5 us -> 9.61 us  [on_device(): lax.all_to_all(send, 'band', 0, 0, tiled=True).reshape(high, plan.piece)]
    unnamed x14 -> x16, local copies, waits for them, and re-layouts: 3.58 us -> 1.34 us
    add x4 -> x0, other arithmetic: 1.3 us -> none  [total_over(): values + lax.ppermute(values, axis, [(i, i ^ bit) for i in range(count)])]
    pallas_call x1, Pallas kernels: 2.35 us -> 1.67 us  [on_device(): pl.pallas_call(functools.partial(last_kernel, plan), out_shape=jax.ShapeD...]
  transfers between devices with their start and end apart: 5 -> 1, of which waited for: 5 -> 1; matrix products, arithmetic and copies ran while one was open for 5% -> 0% of each run, Pallas kernels for 14% -> 12%
where the time goes in v2:
time: 42.8 us; the launch traced here: 42.5 us
  Pallas kernels  13.1 us (31%)
  blocking collectives  10.8 us (25%)
  waiting for transfers between devices  9.61 us (22%)
  starting transfers between devices  7.56 us (18%)
  local copies, waits for them, and re-layouts  1.34 us (3%)
    all_to_all x1, blocking collectives, on_device(): sums = lax.all_to_all(sums, 'band', 0, 0, tiled=True)  10.8 us
    all_to_all x1, waiting for transfers between devices, on_device(): lax.all_to_all(send, 'band', 0, 0, tiled=True).reshape(high, plan.piece)  9.61 us
    all_to_all x1, starting transfers between devices, on_device(): lax.all_to_all(send, 'band', 0, 0, tiled=True).reshape(high, plan.piece)  7.56 us
    pallas_call x1, Pallas kernels, on_device(): pl.pallas_call(functools.partial(bank_kernel, plan), out_shape=[bank(kern...  5.06 us
    pallas_call x1, Pallas kernels, on_device(): pl.pallas_call(functools.partial(main_kernel, plan), out_shape=[pltpu.VME...  4.44 us
    pallas_call x1, Pallas kernels, on_device(): pl.pallas_call(functools.partial(send_kernel, plan), out_shape=pltpu.VMEM...  1.95 us
    pallas_call x1, Pallas kernels, on_device(): pl.pallas_call(functools.partial(last_kernel, plan), out_shape=jax.ShapeD...  1.67 us
    unnamed x16, local copies, waits for them, and re-layouts  1.34 us
  transfers between devices with their start and end apart: 1, of which 1 were waited for; matrix products, arithmetic and copies ran while one was open for 0% of the time, Pallas kernels for 12%

profile of v2, /device:TPU:0, one launch (start us, length us, event | category | flops | bytes accessed | tf_op | source)
XLA Modules:
  0.0 42.5 jit_solution(11373717317692610148)
XLA Ops:
  0.0 1.9 %shard_map.91 = bf16[16,16,1152]{2,1,0:T(8,128)(2,1)} custom-call(bf16[16,16384]{1,0:T(8,128)(2,1)} %design.1), custom_call_target="tpu_custom_call" | custom-call | tf_op jit(solution)/shard_map/pallas_call | solution.py:232
  2.0 0.0 copy-start.3
  2.0 0.0 copy-start.4
  2.0 0.0 copy-start.6
  2.0 7.6 %all-to-all-start = ((bf16[16,16,1152]{2,1,0:T(8,128)(2,1)}), bf16[16,16,1152]{2,1,0:T(8,128)(2,1)S(1)}, u32[]{:S(2)}, u32[]{:S(2)}) async-start(bf16[16,16,1152]{2,1,0:T(8,128)(2,1)} %shard_map.91), calls=%async_computation | async-start | bytes 1179648 | tf_op jit(solution)/shard_map/all_to_all | solution.py:240
  9.6 0.0 copy-start.2
  9.6 0.0 copy-start.5
  9.6 0.0 copy-done.3
  9.6 0.0 copy-done.4
  9.6 0.0 copy-done.6
  9.6 0.6 %copy-done.2 = bf16[8,33]{1,0:T(8,128)(2,1)S(1)} copy-done((bf16[8,33]{1,0:T(8,128)(2,1)S(1)}, bf16[8,33]{1,0:T(8,128)(2,1)}, u32[]{:S(2)}) %copy-start.2) | copy-done | bytes 552
  10.2 0.0 copy-done.5
  10.3 0.0 copy-start.1
  10.3 5.1 %shard_map.92 = (bf16[8,192,128]{2,1,0:T(8,128)(2,1)S(1)}, bf16[8,192,128]{2,1,0:T(8,128)(2,1)S(1)}, bf16[2,192,128]{2,1,0:T(8,128)(2,1)S(1)}, bf16[2,192,128]{2,1,0:T(8,128)(2,1)S(1)}) custom-call(bf16[8,33]{1,0:T(8,128)(2,1)S(1)} %copy-done.2, bf16[8,33]{1,0:T(8,128)(2,1)S(1)} %copy-done.3, bf16[8,32]{1,0:T(8,128)(2,1)S(1)} %bitcast.12, ...), custom_call_target="tpu_custom_call" | custom-call | flops 1000000000 | bytes 8000000 | tf_op jit(solution)/shard_map/pallas_call | solution.py:243
  15.3 9.6 %all-to-all-done = bf16[16,16,1152]{2,1,0:T(8,128)(2,1)S(1)} async-done(((bf16[16,16,1152]{2,1,0:T(8,128)(2,1)}), bf16[16,16,1152]{2,1,0:T(8,128)(2,1)S(1)}, u32[]{:S(2)}, u32[]{:S(2)}) %all-to-all-start) | async-done | bytes 589856 | tf_op jit(solution)/shard_map/all_to_all | solution.py:240
  24.9 0.0 copy-start
  24.9 0.0 copy-start.7
  24.9 0.0 copy-done.1
  24.9 0.6 %copy-done = s32[2,1]{0,1:T(1,128)S(1)} copy-done((s32[2,1]{0,1:T(1,128)S(1)}, s32[2,1]{0,1:T(1,128)}, u32[]{:S(2)}) %copy-start) | copy-done | bytes 32
  25.6 0.0 copy-done.7
  25.6 4.4 %shard_map.93 = (f32[256,1024]{1,0:T(8,128)S(1)}, f32[16,2,128]{2,1,0:T(2,128)S(1)}) custom-call(bf16[256,1152]{1,0:T(8,128)(2,1)S(1)} %bitcast.9, bf16[8,192,128]{2,1,0:T(8,128)(2,1)S(1)} %get-tuple-element.11.rows, bf16[8,192,128]{2,1,0:T(8,128)(2,1)S(1)} %get-tuple-element.12.columns, bf16[2,192,128]{2,1,0:T(8,128)(2,1)S(1)} %get-tuple-element.13.up, ...), custom_call_target="tpu_custom_call" | custom-call | flops 4000000000 | bytes 8000000 | tf_op jit(solution)/shard_map/pallas_call | solution.py:252
  30.1 10.8 %all_to_all.10.sums = f32[16,2,128]{2,1,0:T(2,128)S(1)} all-to-all(f32[16,2,128]{2,1,0:T(2,128)S(1)} %get-tuple-element.16), channel_id=1, replica_groups=mesh['swath'=2,'band'=16] {'band'}, dimensions={0} | all-to-all | bytes 32768 | tf_op jit(solution)/shard_map/all_to_all | solution.py:267
  40.8 1.7 %shard_map.94 = bf16[256,1024]{1,0:T(8,128)(2,1)} custom-call(f32[256,1024]{1,0:T(8,128)S(1)} %get-tuple-element.15.filtered, f32[16,2,128]{2,1,0:T(2,128)S(1)} %all_to_all.10.sums, s32[1,2]{1,0:T(1,128)S(1)} %bitcast.11), custom_call_target="tpu_custom_call" | custom-call | tf_op jit(solution)/shard_map/pallas_call | solution.py:268
Async XLA Ops:
  2.0 7.6 %copy-start.3 = (bf16[8,33]{1,0:T(8,128)(2,1)S(1)}, bf16[8,33]{1,0:T(8,128)(2,1)}, u32[]{:S(2)}) copy-start(bf16[8,33]{1,0:T(8,128)(2,1)} %column_taps.1) | copy-start | bytes 1588
  2.0 7.6 %copy-start.4 = (bf16[32,8]{0,1:T(8,128)(2,1)S(1)}, bf16[32,8]{0,1:T(8,128)(2,1)}, u32[]{:S(2)}) copy-start(bf16[32,8]{0,1:T(8,128)(2,1)} %param.13) | copy-start | bytes 1540
  2.0 7.6 %copy-start.6 = (s32[2,2,1]{1,2,0:T(1,128)S(1)}, s32[2,2,1]{1,2,0:T(1,128)}, u32[]{:S(2)}) copy-start(s32[2,2,1]{1,2,0:T(1,128)} %param.15) | copy-start | bytes 52
  2.0 22.9 %all-to-all-start = ((bf16[16,16,1152]{2,1,0:T(8,128)(2,1)}), bf16[16,16,1152]{2,1,0:T(8,128)(2,1)S(1)}, u32[]{:S(2)}, u32[]{:S(2)}) async-start(bf16[16,16,1152]{2,1,0:T(8,128)(2,1)} %shard_map.91), calls=%async_computation | async-start | bytes 1179648 | tf_op jit(solution)/shard_map/all_to_all | solution.py:240
  9.6 0.7 %copy-start.2 = (bf16[8,33]{1,0:T(8,128)(2,1)S(1)}, bf16[8,33]{1,0:T(8,128)(2,1)}, u32[]{:S(2)}) copy-start(bf16[8,33]{1,0:T(8,128)(2,1)} %row_taps.1) | copy-start | bytes 1588
  9.6 0.7 %copy-start.5 = (s32[2,2,1]{1,2,0:T(1,128)S(1)}, s32[2,2,1]{1,2,0:T(1,128)}, u32[]{:S(2)}) copy-start(s32[2,2,1]{1,2,0:T(1,128)} %param.14) | copy-start | bytes 52
  10.3 14.7 %copy-start.1 = (bf16[256,1024]{1,0:T(8,128)(2,1)S(1)}, bf16[256,1024]{1,0:T(8,128)(2,1)}, u32[]{:S(2)}) copy-start(bf16[256,1024]{1,0:T(8,128)(2,1)} %image.1) | copy-start | bytes 1572868
  24.9 0.7 %copy-start = (s32[2,1]{0,1:T(1,128)S(1)}, s32[2,1]{0,1:T(1,128)}, u32[]{:S(2)}) copy-start(s32[2,1]{0,1:T(1,128)} %param.16) | copy-start | bytes 28
  24.9 0.7 %copy-start.7 = (f32[8]{0:T(128)S(1)}, f32[8]{0:T(128)}, u32[]{:S(2)}) copy-start(f32[8]{0:T(128)} %weight.1) | copy-start | bytes 100

commit v3 on v2

--- a/solution.py
+++ b/solution.py
@@ -66,7 +66,9 @@
             out[s, :, strip:] = jnp.where(lane < LANES // 2, after, before)
 
 
-def bank_kernel(plan, row_taps, column_taps, interp, shift, phase, rows, columns, up, across, tap_rows, tap_cols, fine, fine_back):
+def bank_kernel(
+    plan, row_taps, column_taps, interp, shift, phase, weight, care, rows, columns, up, across, scales, tap_rows, tap_cols, fine, fine_back
+):
     wide = 3 * LANES
     for held in (tap_rows, tap_cols, fine, fine_back):
         held[...] = jnp.zeros_like(held)
@@ -104,6 +106,10 @@
     for b in range(plan.blocks):
         fill(up, b, fine[pl.ds(phase[0, 0, b], 1), :], shift[0, 0, b] - middle)
         fill(across, b, fine_back[pl.ds(phase[1, 0, b], 1), :], -shift[1, 0, b])
+    for k in range(plan.kernels):
+        scales[k : k + 1, :] = jnp.full((1, WIN), weight[k], jnp.float32)
+    for b in range(plan.blocks):
+        scales[plan.kernels + b : plan.kernels + b + 1, :] = jnp.full((1, WIN), care[0, b].astype(jnp.float32))
 
 
 def band(bank, at, offset, count, cols, used=None):
@@ -121,7 +127,7 @@
 
 
 def main_kernel(
-    plan, design, rows, columns, up, across, weight, care, image, filtered, sums, ext, chunk, intensity, partial, diff
+    plan, design, rows, columns, up, across, scales, image, filtered, sums, ext, chunk, intensity, partial, diff
 ):
     high, pad, tile = plan.height, plan.pad, plan.tile_rows
     strip = plan.strip
@@ -151,7 +157,7 @@
                     preferred_element_type=f32,
                 ).astype(bf16)
                 field = jnp.dot(smooth, band(columns, k, 1 - plan.reach, WIN, WIN), preferred_element_type=f32)
-                total = total + weight[k] * field * field
+                total = total + scales[k : k + 1, :] * field * field
             intensity[c, pad + tile * r : pad + tile * (r + 1), :] = jnp.where(inside, total, 0.0).astype(bf16)
     for c in range(plan.chunks):
         for b in range(plan.blocks):
@@ -166,7 +172,7 @@
     diff[8 + high :, :] = jnp.zeros((8, strip), f32)
     middle = plan.taps // 2 - 1
     for b in range(plan.blocks):
-        cared = care[0, b].astype(f32)
+        cared = scales[plan.kernels + b : plan.kernels + b + 1, : plan.tile_cols]
         for q in range(plan.col_tiles):
             warped = jnp.zeros((BLK, plan.tile_cols), f32)
             for tile_at, c in plan.pairs:
@@ -194,17 +200,16 @@
         sums[s] = both
 
 
-def last_kernel(plan, filtered, sums, care, out):
+def last_kernel(plan, filtered, sums, scales, out):
     cells = plan.height * plan.width
-    both = jnp.sum(sums[...], axis=0)
-    mean = jnp.sum(both[0:1, :]) / cells
-    variance = jnp.sum(both[1:2, :]) / cells - mean * mean
-    scale = lax.rsqrt(jnp.full((1, LANES), variance + epsilon, jnp.float32))
-    for b in range(plan.blocks):
-        cared = care[0, b].astype(jnp.float32)
-        for at in range(0, plan.strip, LANES):
-            value = filtered[BLK * b : BLK * (b + 1), at : at + LANES]
-            out[BLK * b : BLK * (b + 1), at : at + LANES] = (cared * ((value - mean) * scale)).astype(out.dtype)
+    both = jnp.sum(jnp.sum(sums[...], axis=0), axis=1, keepdims=True)
+    mean = both[0:1] / cells
+    variance = both[1:2] / cells - mean * mean
+    scale = lax.rsqrt(variance + epsilon)
+    for b in range(plan.blocks):
+        factor = scales[plan.kernels + b : plan.kernels + b + 1, 0:1] * scale
+        rows = slice(BLK * b, BLK * (b + 1))
+        out[rows, :] = ((filtered[rows, :] - mean) * factor).astype(out.dtype)
 
 
 VMEM = pl.BlockSpec(memory_space=pltpu.VMEM)
@@ -240,19 +245,22 @@
     got = lax.all_to_all(send, "band", 0, 0, tiled=True).reshape(high, plan.piece)
     bank = lambda count: pltpu.VMEM((count, 16 * TILES, LANES), bf16)
     taps = lambda count: pltpu.VMEM((count, 3 * LANES), f32)
-    rows, columns, up, across = pl.pallas_call(
+    rows, columns, up, across, scales = pl.pallas_call(
         functools.partial(bank_kernel, plan),
-        out_shape=[bank(kernels), bank(kernels), bank(plan.blocks), bank(plan.blocks)],
-        in_specs=[VMEM, VMEM, VMEM, SMEM, SMEM],
-        out_specs=[VMEM] * 4,
+        out_shape=[bank(kernels), bank(kernels), bank(plan.blocks), bank(plan.blocks), pltpu.VMEM((kernels + plan.blocks, WIN), f32)],
+        in_specs=[VMEM, VMEM, VMEM, SMEM, SMEM, SMEM, SMEM],
+        out_specs=[VMEM] * 5,
         scratch_shapes=[taps(kernels), taps(kernels), taps(interp.shape[0]), taps(interp.shape[0])],
         compiler_params=GRANT,
         cost_estimate=pl.CostEstimate(flops=10**9, bytes_accessed=8 * 10**6, transcendentals=0),
-    )(row_taps, column_taps, interp.T, jnp.swapaxes(block_shift, 1, 2), jnp.swapaxes(block_phase, 1, 2))
+    )(
+        row_taps, column_taps, interp.T, jnp.swapaxes(block_shift, 1, 2), jnp.swapaxes(block_phase, 1, 2),
+        kernel_weight, care.T,
+    )
     filtered, sums = pl.pallas_call(
         functools.partial(main_kernel, plan),
         out_shape=[pltpu.VMEM((high, strip), f32), pltpu.VMEM((plan.devices, 2, LANES), f32)],
-        in_specs=[VMEM] * 5 + [SMEM, SMEM, VMEM],
+        in_specs=[VMEM] * 7,
         out_specs=[VMEM] * 2,
         scratch_shapes=[
             pltpu.VMEM((high + 2 * plan.pad, plan.ext), bf16),
@@ -263,15 +271,15 @@
         ],
         compiler_params=GRANT,
         cost_estimate=pl.CostEstimate(flops=4 * 10**9, bytes_accessed=8 * 10**6, transcendentals=0),
-    )(near(got), near(rows), near(columns), near(up), near(across), kernel_weight, care.T, near(image))
+    )(near(got), near(rows), near(columns), near(up), near(across), near(scales), near(image))
     sums = lax.all_to_all(sums, "band", 0, 0, tiled=True)
     return pl.pallas_call(
         functools.partial(last_kernel, plan),
         out_shape=jax.ShapeDtypeStruct((high, strip), bf16),
-        in_specs=[VMEM, VMEM, SMEM],
+        in_specs=[VMEM, VMEM, VMEM],
         out_specs=VMEM,
         compiler_params=GRANT,
-    )(near(filtered), near(sums), care.T)
+    )(near(filtered), near(sums), near(scales))
 
 
 def solution(mesh):

time: 42.8 us -> 41 us (0.958)
  Pallas kernels: 13.1 us -> 12 us
  local copies, waits for them, and re-layouts: 1.34 us -> 0.66 us
    unnamed x16, local copies, waits for them, and re-layouts: 1.34 us -> 0.66 us
    pallas_call x1, Pallas kernels: 1.67 us -> 1.08 us  [on_device(): pl.pallas_call(functools.partial(last_kernel, plan), out_shape=jax.ShapeD...]
    pallas_call x1, Pallas kernels: 4.44 us -> 3.86 us  [on_device(): pl.pallas_call(functools.partial(main_kernel, plan), out_shape=[pltpu.VME...]
where the time goes in v3:
time: 41 us; the launch traced here: 40.7 us
  Pallas kernels  12 us (29%)
  blocking collectives  10.8 us (26%)
  waiting for transfers between devices  9.58 us (23%)
  starting transfers between devices  7.56 us (18%)
  local copies, waits for them, and re-layouts  0.66 us (2%)
    all_to_all x1, blocking collectives, on_device(): sums = lax.all_to_all(sums, 'band', 0, 0, tiled=True)  10.8 us
    all_to_all x1, waiting for transfers between devices, on_device(): lax.all_to_all(send, 'band', 0, 0, tiled=True).reshape(high, plan.piece)  9.58 us
    all_to_all x1, starting transfers between devices, on_device(): lax.all_to_all(send, 'band', 0, 0, tiled=True).reshape(high, plan.piece)  7.56 us
    pallas_call x1, Pallas kernels, on_device(): pl.pallas_call(functools.partial(bank_kernel, plan), out_shape=[bank(kern...  5.08 us
    pallas_call x1, Pallas kernels, on_device(): pl.pallas_call(functools.partial(main_kernel, plan), out_shape=[pltpu.VME...  3.86 us
    pallas_call x1, Pallas kernels, on_device(): pl.pallas_call(functools.partial(send_kernel, plan), out_shape=pltpu.VMEM...  1.95 us
    pallas_call x1, Pallas kernels, on_device(): pl.pallas_call(functools.partial(last_kernel, plan), out_shape=jax.ShapeD...  1.08 us
  transfers between devices with their start and end apart: 1, of which 1 were waited for; matrix products, arithmetic and copies ran while one was open for 0% of the time, Pallas kernels for 12%

profile of v3, /device:TPU:0, one launch (start us, length us, event | category | flops | bytes accessed | tf_op | source)
XLA Modules:
  0.0 40.7 jit_solution(12005493928941578792)
XLA Ops:
  0.0 1.9 %shard_map.91 = bf16[16,16,1152]{2,1,0:T(8,128)(2,1)} custom-call(bf16[16,16384]{1,0:T(8,128)(2,1)} %design.1), custom_call_target="tpu_custom_call" | custom-call | tf_op jit(solution)/shard_map/pallas_call | solution.py:237
  2.0 0.0 copy-start.2
  2.0 0.0 copy-start.3
  2.0 0.0 copy-start.5
  2.0 0.0 copy-start.7
  2.0 7.6 %all-to-all-start = ((bf16[16,16,1152]{2,1,0:T(8,128)(2,1)}), bf16[16,16,1152]{2,1,0:T(8,128)(2,1)S(1)}, u32[]{:S(2)}, u32[]{:S(2)}) async-start(bf16[16,16,1152]{2,1,0:T(8,128)(2,1)} %shard_map.91), calls=%async_computation | async-start | bytes 1179648 | tf_op jit(solution)/shard_map/all_to_all | solution.py:245
  9.6 0.0 copy-start.1
  9.6 0.0 copy-start.4
  9.6 0.0 copy-start.6
  9.6 0.0 copy-done.2
  9.6 0.0 copy-done.3
  9.6 0.0 copy-done.5
  9.6 0.0 copy-done.7
  9.6 0.6 %copy-done.1 = bf16[8,33]{1,0:T(8,128)(2,1)S(1)} copy-done((bf16[8,33]{1,0:T(8,128)(2,1)S(1)}, bf16[8,33]{1,0:T(8,128)(2,1)}, u32[]{:S(2)}) %copy-start.1) | copy-done | bytes 552
  10.3 0.0 copy-done.4
  10.3 0.0 copy-done.6
  10.3 0.0 copy-start
  10.3 5.1 %shard_map.92 = (bf16[8,192,128]{2,1,0:T(8,128)(2,1)S(1)}, bf16[8,192,128]{2,1,0:T(8,128)(2,1)S(1)}, bf16[2,192,128]{2,1,0:T(8,128)(2,1)S(1)}, bf16[2,192,128]{2,1,0:T(8,128)(2,1)S(1)}, f32[10,256]{1,0:T(8,128)S(1)}) custom-call(bf16[8,33]{1,0:T(8,128)(2,1)S(1)} %copy-done.1, bf16[8,33]{1,0:T(8,128)(2,1)S(1)} %copy-done.2, bf16[8,32]{1,0:T(8,128)(2,1)S(1)} %bitcast.10, ...), custom_call_target="tpu_custom_call" | custom-call | flops 1000000000 | bytes 8000000 | tf_op jit(solution)/shard_map/pallas_call | solution.py:248
  15.4 9.6 %all-to-all-done = bf16[16,16,1152]{2,1,0:T(8,128)(2,1)S(1)} async-done(((bf16[16,16,1152]{2,1,0:T(8,128)(2,1)}), bf16[16,16,1152]{2,1,0:T(8,128)(2,1)S(1)}, u32[]{:S(2)}, u32[]{:S(2)}) %all-to-all-start) | async-done | bytes 589856 | tf_op jit(solution)/shard_map/all_to_all | solution.py:245
  24.9 0.0 copy-done
  24.9 3.9 %shard_map.93 = (f32[256,1024]{1,0:T(8,128)S(1)}, f32[16,2,128]{2,1,0:T(2,128)S(1)}) custom-call(bf16[256,1152]{1,0:T(8,128)(2,1)S(1)} %bitcast.9, bf16[8,192,128]{2,1,0:T(8,128)(2,1)S(1)} %get-tuple-element.12.rows, bf16[8,192,128]{2,1,0:T(8,128)(2,1)S(1)} %get-tuple-element.13.columns, bf16[2,192,128]{2,1,0:T(8,128)(2,1)S(1)} %get-tuple-element.14.up, ...), custom_call_target="tpu_custom_call" | custom-call | flops 4000000000 | bytes 8000000 | tf_op jit(solution)/shard_map/pallas_call | solution.py:260
  28.8 10.8 %all_to_all.10.sums = f32[16,2,128]{2,1,0:T(2,128)S(1)} all-to-all(f32[16,2,128]{2,1,0:T(2,128)S(1)} %get-tuple-element.18), channel_id=1, replica_groups=mesh['swath'=2,'band'=16] {'band'}, dimensions={0} | all-to-all | bytes 32768 | tf_op jit(solution)/shard_map/all_to_all | solution.py:275
  39.6 1.1 %shard_map.94 = bf16[256,1024]{1,0:T(8,128)(2,1)} custom-call(f32[256,1024]{1,0:T(8,128)S(1)} %get-tuple-element.17.filtered, f32[16,2,128]{2,1,0:T(2,128)S(1)} %all_to_all.10.sums, f32[10,256]{1,0:T(8,128)S(1)} %get-tuple-element.16.scales), custom_call_target="tpu_custom_call" | custom-call | tf_op jit(solution)/shard_map/pallas_call | solution.py:276
Async XLA Ops:
  2.0 7.7 %copy-start.2 = (bf16[8,33]{1,0:T(8,128)(2,1)S(1)}, bf16[8,33]{1,0:T(8,128)(2,1)}, u32[]{:S(2)}) copy-start(bf16[8,33]{1,0:T(8,128)(2,1)} %column_taps.1) | copy-start | bytes 1588
  2.0 7.7 %copy-start.3 = (bf16[32,8]{0,1:T(8,128)(2,1)S(1)}, bf16[32,8]{0,1:T(8,128)(2,1)}, u32[]{:S(2)}) copy-start(bf16[32,8]{0,1:T(8,128)(2,1)} %param.13) | copy-start | bytes 1540
  2.0 7.6 %copy-start.5 = (s32[2,2,1]{1,2,0:T(1,128)S(1)}, s32[2,2,1]{1,2,0:T(1,128)}, u32[]{:S(2)}) copy-start(s32[2,2,1]{1,2,0:T(1,128)} %param.15) | copy-start | bytes 52
  2.0 7.6 %copy-start.7 = (s32[2,1]{0,1:T(1,128)S(1)}, s32[2,1]{0,1:T(1,128)}, u32[]{:S(2)}) copy-start(s32[2,1]{0,1:T(1,128)} %param.16) | copy-start | bytes 28
  2.0 22.9 %all-to-all-start = ((bf16[16,16,1152]{2,1,0:T(8,128)(2,1)}), bf16[16,16,1152]{2,1,0:T(8,128)(2,1)S(1)}, u32[]{:S(2)}, u32[]{:S(2)}) async-start(bf16[16,16,1152]{2,1,0:T(8,128)(2,1)} %shard_map.91), calls=%async_computation | async-start | bytes 1179648 | tf_op jit(solution)/shard_map/all_to_all | solution.py:245
  9.6 0.7 %copy-start.1 = (bf16[8,33]{1,0:T(8,128)(2,1)S(1)}, bf16[8,33]{1,0:T(8,128)(2,1)}, u32[]{:S(2)}) copy-start(bf16[8,33]{1,0:T(8,128)(2,1)} %row_taps.1) | copy-start | bytes 1588
  9.6 0.7 %copy-start.4 = (s32[2,2,1]{1,2,0:T(1,128)S(1)}, s32[2,2,1]{1,2,0:T(1,128)}, u32[]{:S(2)}) copy-start(s32[2,2,1]{1,2,0:T(1,128)} %param.14) | copy-start | bytes 52
  9.6 0.7 %copy-start.6 = (f32[8]{0:T(128)S(1)}, f32[8]{0:T(128)}, u32[]{:S(2)}) copy-start(f32[8]{0:T(128)} %weight.1) | copy-start | bytes 100
  10.3 14.7 %copy-start = (bf16[256,1024]{1,0:T(8,128)(2,1)S(1)}, bf16[256,1024]{1,0:T(8,128)(2,1)}, u32[]{:S(2)}) copy-start(bf16[256,1024]{1,0:T(8,128)(2,1)} %image.1) | copy-start | bytes 1572868

commit v4 on v3

--- a/solution.py
+++ b/solution.py
@@ -7,11 +7,13 @@
 from jax.experimental.pallas import tpu as pltpu
 from jax.sharding import PartitionSpec as P
 
+
 BLK = 128
 P_SIZE = 28
 LANES = 128
 WIN = 256
 ZERO = 160
+CORES = 2
 TILES = 12
 
 epsilon = 1e-05
@@ -40,36 +42,67 @@
             first = (self.tile_cols * q + 1) // self.step
             last = min((self.tile_cols * (q + 1) - 1 + 2 * P_SIZE) // self.step, self.chunks - 1)
             self.pairs += [(q, c) for c in range(first, last + 1)]
-        self.parts = 4 if devices % 4 == 0 else 1
+        self.chips = devices // CORES
+        self.union = CORES * self.strip + LANES
         self.ext = pl.cdiv(LANES + self.step * self.chunks + WIN, LANES) * LANES
 
 
-def send_kernel(plan, design, out, held, arrived):
+def partner(chip, hop, chips, back=False):
+    if chips & (chips - 1) == 0:
+        return chip ^ hop
+    return (chip - hop + chips) % chips if back else (chip + hop) % chips
+
+
+def send_kernel(plan, design, *rest):
+    count = (len(rest) - plan.chips - 2) // 2
+    small, outs, small_outs = rest[:count], rest[count : count + plan.chips], rest[count + plan.chips : -2]
+    held, arrived = rest[-2:]
     lane = lax.broadcasted_iota(jnp.int32, (plan.rows_dev, LANES), 1)
-    zero = jnp.zeros((plan.rows_dev, LANES), out.dtype)
-    strip, part = plan.strip, plan.width // plan.parts
-    copies = [
-        pltpu.make_async_copy(design.at[:, pl.ds(i * part, part)], held.at[:, pl.ds(i * part, part)], arrived.at[i])
-        for i in range(plan.parts)
+    chip = lax.axis_index("band") // CORES
+    copy = pltpu.make_async_copy(design, held.at[:, LANES : LANES + plan.width], arrived.at[0])
+    copy.start()
+    others = [
+        pltpu.make_async_copy(source, out, arrived.at[i + 1]) for i, (source, out) in enumerate(zip(small, small_outs))
     ]
-    for copy in copies:
-        copy.start()
-    for i in range(plan.parts):
-        copies[i].wait()
-        each = plan.devices // plan.parts
-        for s in range(i * each, (i + 1) * each):
-            out[s, :, :strip] = held[:, s * strip : (s + 1) * strip]
-        for s in range(max(i * each - 1, 0), plan.devices if i == plan.parts - 1 else (i + 1) * each - 1):
-            at = s * strip
-            before = held[:, at - LANES : at] if s else zero
-            after = held[:, at + strip : at + strip + LANES] if s < plan.devices - 1 else zero
-            out[s, :, strip:] = jnp.where(lane < LANES // 2, after, before)
+    for other in others:
+        other.start()
+    held[:, :LANES] = jnp.zeros((plan.rows_dev, LANES), held.dtype)
+    held[:, LANES + plan.width :] = jnp.zeros((plan.rows_dev, LANES), held.dtype)
+    copy.wait()
+    both = CORES * plan.strip
+    for hop, out in enumerate(outs):
+        at = pl.multiple_of(partner(chip, hop, plan.chips) * both, LANES)
+        out[:, :both] = held[:, pl.ds(at + LANES, both)]
+        before = held[:, pl.ds(at, LANES)]
+        after = held[:, pl.ds(at + LANES + both, LANES)]
+        out[:, both:] = jnp.where(lane < LANES // 2, after, before)
+    for other in others:
+        other.wait()
+
+
+def strip_of(plan, union, core):
+    lane = lax.broadcasted_iota(jnp.int32, (plan.rows_dev, LANES), 1)
+    strip = plan.strip
+    own = union[:, pl.ds(pl.multiple_of(core * strip, LANES), strip)]
+    rim = union[:, CORES * strip :]
+    first = jnp.where(lane < LANES // 2, union[:, strip : strip + LANES], rim)
+    second = jnp.where(lane < LANES // 2, rim, union[:, strip - LANES : strip])
+    return own, jnp.where(core == 0, first, second)
+
+
+def swap_kernel(plan, *rest):
+    unions, out = rest[: plan.chips], rest[plan.chips]
+    other = CORES - 1 - lax.rem(lax.axis_index("band"), CORES)
+    for hop, union in enumerate(unions):
+        own, rims = strip_of(plan, union, other)
+        rows = slice(plan.rows_dev * hop, plan.rows_dev * (hop + 1))
+        out[rows, : plan.strip] = own
+        out[rows, plan.strip :] = rims
 
 
 def bank_kernel(
     plan, row_taps, column_taps, interp, shift, phase, weight, care, rows, columns, up, across, scales, tap_rows, tap_cols, fine, fine_back
 ):
-    wide = 3 * LANES
     for held in (tap_rows, tap_cols, fine, fine_back):
         held[...] = jnp.zeros_like(held)
     tap_rows[:, : plan.reach] = row_taps[...].astype(jnp.float32)
@@ -84,32 +117,52 @@
             values.astype(jnp.bfloat16), chosen, (((side,), (0,)), ((), ())), preferred_element_type=jnp.float32
         )
 
-    tap_cols[:, :LANES] = pick(tap_cols[:, :LANES], 1, plan.reach - 1)
-    fine[:, :LANES] = pick(interp[...], 0)
-    fine_back[:, :LANES] = pick(interp[...], 0, plan.taps - 1)
-    row = lax.broadcasted_iota(jnp.int32, (16, wide), 0)
-
-    def fill(bank, at, taps, moved):
-        base = pltpu.roll(jnp.broadcast_to(taps, (16, wide)), ZERO + moved, 1)
+    tap_cols[...] = pick(tap_cols[...], 1, plan.reach - 1)
+    fine[...] = pick(interp[...], 0)
+    fine_back[...] = pick(interp[...], 0, plan.taps - 1)
+    row = lax.broadcasted_iota(jnp.int32, (16, LANES), 0)
+    lane = lax.broadcasted_iota(jnp.int32, (16, LANES), 1)
+
+    def fill(bank, at, taps, moved=None):
+        base = jnp.broadcast_to(taps, (16, LANES))
+        if moved is None:
+            base = pltpu.roll(base, ZERO - LANES, 1)
+        else:
+            ahead = jnp.broadcast_to(moved + (ZERO - LANES), (16, LANES))
+            for bit in (1, 2, 4, 8, 16, 32):
+                base = jnp.where((ahead & bit) != 0, pltpu.roll(base, bit, 1), base)
         for bit in (1, 2, 4, 8):
             base = jnp.where((row & bit) != 0, pltpu.roll(base, bit, 1), base)
         for m in range(TILES):
-            bank[at, 16 * m : 16 * (m + 1), :] = base[:, 16 * (m + 1) : 16 * (m + 1) + LANES].astype(jnp.bfloat16)
+            start = LANES - 16 * (m + 1)
+            tile = pltpu.roll(base, start % LANES, 1)
+            tile = jnp.where(lane >= start if start >= 0 else lane < LANES + start, tile, 0.0)
+            bank[at, 16 * m : 16 * (m + 1), :] = tile.astype(jnp.bfloat16)
 
     def per_kernel(k, carry):
-        fill(rows, k, tap_rows[pl.ds(k, 1), :], 0)
-        fill(columns, k, tap_cols[pl.ds(k, 1), :], 0)
+        fill(rows, k, tap_rows[pl.ds(k, 1), :])
+        fill(columns, k, tap_cols[pl.ds(k, 1), :])
         return carry
 
     lax.fori_loop(0, plan.kernels, per_kernel, 0)
+
+    def column(line):
+        count = line.shape[1]
+        a = lax.broadcasted_iota(jnp.int32, (count, count), 0)
+        b = lax.broadcasted_iota(jnp.int32, (count, count), 1)
+        return jnp.sum(jnp.where(a == b, jnp.broadcast_to(line, (count, count)), 0.0), axis=1, keepdims=True)
+
     middle = plan.taps // 2 - 1
-    for b in range(plan.blocks):
-        fill(up, b, fine[pl.ds(phase[0, 0, b], 1), :], shift[0, 0, b] - middle)
-        fill(across, b, fine_back[pl.ds(phase[1, 0, b], 1), :], -shift[1, 0, b])
-    for k in range(plan.kernels):
-        scales[k : k + 1, :] = jnp.full((1, WIN), weight[k], jnp.float32)
-    for b in range(plan.blocks):
-        scales[plan.kernels + b : plan.kernels + b + 1, :] = jnp.full((1, WIN), care[0, b].astype(jnp.float32))
+    phases = lax.broadcasted_iota(jnp.int32, (plan.blocks, interp.shape[1]), 1).astype(jnp.float32)
+    for axis, (held, bank) in enumerate(((fine, up), (fine_back, across))):
+        chosen = jnp.where(phases == column(phase[axis].astype(jnp.float32)), 1.0, 0.0).astype(jnp.bfloat16)
+        taps = jnp.dot(chosen, held[...].astype(jnp.bfloat16), preferred_element_type=jnp.float32)
+        moved = column(shift[axis].astype(jnp.float32)).astype(jnp.int32)
+        for b in range(plan.blocks):
+            by = moved[b : b + 1]
+            fill(bank, b, taps[b : b + 1], by - middle if axis == 0 else -by)
+    scales[: plan.kernels, :] = jnp.broadcast_to(column(weight[...]), (plan.kernels, WIN))
+    scales[plan.kernels :, :] = jnp.broadcast_to(column(care[...].astype(jnp.float32)), (plan.blocks, WIN))
 
 
 def band(bank, at, offset, count, cols, used=None):
@@ -127,8 +180,10 @@
 
 
 def main_kernel(
-    plan, design, rows, columns, up, across, scales, image, filtered, sums, ext, chunk, intensity, partial, diff
+    plan, *rest
 ):
+    unions, rest = rest[: plan.chips], rest[plan.chips :]
+    swapped, rows, columns, up, across, scales, image, filtered, sums, ext, chunk, intensity, partial, diff = rest
     high, pad, tile = plan.height, plan.pad, plan.tile_rows
     strip = plan.strip
     bf16, f32 = jnp.bfloat16, jnp.float32
@@ -138,9 +193,17 @@
         intensity[...] = jnp.zeros_like(intensity)
     elif plan.ext > strip + 2 * LANES:
         ext[:, strip + 2 * LANES :] = jnp.zeros((high, plan.ext - strip - 2 * LANES), ext.dtype)
-    ext[pad : pad + high, :LANES] = design[:, strip:]
-    ext[pad : pad + high, LANES : LANES + strip] = design[:, :strip]
-    ext[pad : pad + high, LANES + strip : 2 * LANES + strip] = design[:, strip:]
+    chip, core = place // CORES, lax.rem(place, CORES)
+    each = plan.rows_dev
+    for hop in range(plan.chips):
+        source = partner(chip, hop, plan.chips, True) * CORES
+        own, rims = strip_of(plan, unions[hop], core)
+        there = swapped[each * hop : each * (hop + 1), :]
+        for values, edge, of in ((own, rims, core), (there[:, :strip], there[:, strip:], CORES - 1 - core)):
+            at = pl.ds(pl.multiple_of(pad + (source + of) * each, 16), each)
+            ext[at, :LANES] = edge
+            ext[at, LANES : LANES + strip] = values
+            ext[at, LANES + strip : 2 * LANES + strip] = edge
     for c in range(plan.chunks):
         at = LANES - plan.lead + plan.step * c
         chunk[c] = ext[:, at : at + WIN]
@@ -226,6 +289,10 @@
     return pltpu.with_memory_space_constraint(value, pltpu.HBM)
 
 
+def hops(chips):
+    return sorted(range(1, chips), key=lambda hop: (-hop.bit_length(), hop))
+
+
 def on_device(
     design, row_taps, column_taps, kernel_weight, interp, block_shift, block_phase, care, image
 ):
@@ -234,33 +301,58 @@
     )
     bf16, f32 = jnp.bfloat16, jnp.float32
     high, strip, kernels = plan.height, plan.strip, plan.kernels
-    send = pl.pallas_call(
+    chips, both = plan.chips, plan.union
+    small = (
+        row_taps, column_taps, interp.T, jnp.swapaxes(block_shift, 1, 2), jnp.swapaxes(block_phase, 1, 2),
+        kernel_weight[None], care.T,
+    )
+    sent = pl.pallas_call(
         functools.partial(send_kernel, plan),
-        out_shape=pltpu.VMEM((plan.devices, plan.rows_dev, plan.piece), bf16),
-        in_specs=[FAR],
+        out_shape=[pltpu.VMEM((plan.rows_dev, both), bf16)] * chips
+        + [pltpu.VMEM(value.shape, value.dtype) for value in small],
+        in_specs=[FAR] * (1 + len(small)),
+        out_specs=[VMEM] * (chips + len(small)),
+        scratch_shapes=[
+            pltpu.VMEM((plan.rows_dev, plan.width + 2 * LANES), bf16),
+            pltpu.SemaphoreType.DMA((1 + len(small),)),
+        ],
+        compiler_params=GRANT,
+    )(far(design), *[far(value) for value in small])
+    unions, small = list(sent[:chips]), sent[chips:]
+    for hop in hops(chips):
+        pairs = [
+            (CORES * chip + core, CORES * partner(chip, hop, chips) + core)
+            for chip in range(chips)
+            for core in range(CORES)
+        ]
+        unions[hop] = lax.ppermute(unions[hop], "band", pairs)
+    unions = [near(union) for union in unions]
+    swapped = pl.pallas_call(
+        functools.partial(swap_kernel, plan),
+        out_shape=pltpu.VMEM((chips * plan.rows_dev, plan.piece), bf16),
+        in_specs=[VMEM] * chips,
         out_specs=VMEM,
-        scratch_shapes=[pltpu.VMEM(design.shape, bf16), pltpu.SemaphoreType.DMA((plan.parts,))],
-        compiler_params=GRANT,
-    )(far(design))
-    got = lax.all_to_all(send, "band", 0, 0, tiled=True).reshape(high, plan.piece)
+        compiler_params=GRANT,
+    )(*unions)
+    swapped = lax.ppermute(swapped, "band", [(i, i ^ 1) for i in range(plan.devices)])
     bank = lambda count: pltpu.VMEM((count, 16 * TILES, LANES), bf16)
-    taps = lambda count: pltpu.VMEM((count, 3 * LANES), f32)
+    taps = lambda count: pltpu.VMEM((count, LANES), f32)
     rows, columns, up, across, scales = pl.pallas_call(
         functools.partial(bank_kernel, plan),
-        out_shape=[bank(kernels), bank(kernels), bank(plan.blocks), bank(plan.blocks), pltpu.VMEM((kernels + plan.blocks, WIN), f32)],
-        in_specs=[VMEM, VMEM, VMEM, SMEM, SMEM, SMEM, SMEM],
+        out_shape=[
+            bank(kernels), bank(kernels), bank(plan.blocks), bank(plan.blocks),
+            pltpu.VMEM((kernels + plan.blocks, WIN), f32),
+        ],
+        in_specs=[VMEM] * 7,
         out_specs=[VMEM] * 5,
         scratch_shapes=[taps(kernels), taps(kernels), taps(interp.shape[0]), taps(interp.shape[0])],
         compiler_params=GRANT,
         cost_estimate=pl.CostEstimate(flops=10**9, bytes_accessed=8 * 10**6, transcendentals=0),
-    )(
-        row_taps, column_taps, interp.T, jnp.swapaxes(block_shift, 1, 2), jnp.swapaxes(block_phase, 1, 2),
-        kernel_weight, care.T,
-    )
+    )(*[near(value) for value in small])
     filtered, sums = pl.pallas_call(
         functools.partial(main_kernel, plan),
         out_shape=[pltpu.VMEM((high, strip), f32), pltpu.VMEM((plan.devices, 2, LANES), f32)],
-        in_specs=[VMEM] * 7,
+        in_specs=[VMEM] * (chips + 7),
         out_specs=[VMEM] * 2,
         scratch_shapes=[
             pltpu.VMEM((high + 2 * plan.pad, plan.ext), bf16),
@@ -271,7 +363,7 @@
         ],
         compiler_params=GRANT,
         cost_estimate=pl.CostEstimate(flops=4 * 10**9, bytes_accessed=8 * 10**6, transcendentals=0),
-    )(near(got), near(rows), near(columns), near(up), near(across), near(scales), near(image))
+    )(*unions, near(swapped), near(rows), near(columns), near(up), near(across), near(scales), near(image))
     sums = lax.all_to_all(sums, "band", 0, 0, tiled=True)
     return pl.pallas_call(
         functools.partial(last_kernel, plan),

time: 41 us -> 41.9 us (1.022)
  starting transfers between devices: 7.56 us -> 12.6 us
  waiting for transfers between devices: 9.58 us -> 7.1 us
  Pallas kernels: 12 us -> 10.8 us
  local copies, waits for them, and re-layouts: 0.66 us -> 0.01 us
    ppermute x0 -> x8, starting transfers between devices: none -> 12.6 us  [the longest x7 12.5 us: on_device(): unions[hop] = lax.ppermute(unions[hop], 'band', pairs)]
    all_to_all x1 -> x0, waiting for transfers between devices: 9.58 us -> none  [on_device(): lax.all_to_all(send, 'band', 0, 0, tiled=True).reshape(high, plan.piece)]
    all_to_all x1 -> x0, starting transfers between devices: 7.56 us -> none  [on_device(): lax.all_to_all(send, 'band', 0, 0, tiled=True).reshape(high, plan.piece)]
    ppermute x0 -> x8, waiting for transfers between devices: none -> 7.1 us  [the longest x7 7.1 us: on_device(): unions[hop] = lax.ppermute(unions[hop], 'band', pairs)]
    pallas_call x1 -> x2, Pallas kernels: 1.95 us -> 1.21 us  [the longest x1 1.17 us: on_device(): pl.pallas_call(functools.partial(send_kernel, plan), out_shape=[pltpu.VME...]
    unnamed x16 -> x2, local copies, waits for them, and re-layouts: 0.66 us -> 0.01 us
    pallas_call x1, Pallas kernels: 5.08 us -> 4.63 us  [on_device(): pl.pallas_call(functools.partial(bank_kernel, plan), out_shape=[bank(kern...]
    all_to_all x1, blocking collectives: 10.8 us -> 11.2 us  [on_device(): sums = lax.all_to_all(sums, 'band', 0, 0, tiled=True)]
  transfers between devices with their start and end apart: 1 -> 8, of which waited for: 1 -> 2; matrix products, arithmetic and copies ran while one was open for 0% -> 0% of each run, Pallas kernels for 12% -> 11%
where the time goes in v4:
time: 41.9 us; the launch traced here: 41.8 us
  starting transfers between devices  12.6 us (30%)
  blocking collectives  11.2 us (27%)
  Pallas kernels  10.8 us (26%)
  waiting for transfers between devices  7.1 us (17%)
    ppermute x7, starting transfers between devices, on_device(): unions[hop] = lax.ppermute(unions[hop], 'band', pairs)  12.5 us
    all_to_all x1, blocking collectives, on_device(): sums = lax.all_to_all(sums, 'band', 0, 0, tiled=True)  11.2 us
    ppermute x7, waiting for transfers between devices, on_device(): unions[hop] = lax.ppermute(unions[hop], 'band', pairs)  7.1 us
    pallas_call x1, Pallas kernels, on_device(): pl.pallas_call(functools.partial(bank_kernel, plan), out_shape=[bank(kern...  4.63 us
    pallas_call x1, Pallas kernels, on_device(): pl.pallas_call(functools.partial(main_kernel, plan), out_shape=[pltpu.VME...  3.88 us
    pallas_call x1, Pallas kernels, on_device(): pl.pallas_call(functools.partial(send_kernel, plan), out_shape=[pltpu.VME...  1.17 us
    pallas_call x1, Pallas kernels, on_device(): pl.pallas_call(functools.partial(last_kernel, plan), out_shape=jax.ShapeD...  1.08 us
  transfers between devices with their start and end apart: 8, of which 2 were waited for; matrix products, arithmetic and copies ran while one was open for 0% of the time, Pallas kernels for 11%

profile of v4, /device:TPU:0, one launch (start us, length us, event | category | flops | bytes accessed | tf_op | source)
XLA Modules:
  0.0 41.8 jit_solution(6346291060742372505)
XLA Ops:
  0.0 1.2 %shard_map.91 = (bf16[16,2176]{1,0:T(8,128)(2,1)S(1)}, bf16[16,2176]{1,0:T(8,128)(2,1)S(1)}, bf16[16,2176]{1,0:T(8,128)(2,1)S(1)}, bf16[16,2176]{1,0:T(8,128)(2,...) custom-call(bf16[16,16384]{1,0:T(8,128)(2,1)} %design.1, ...), custom_call_target="tpu_custom_call" | custom-call | tf_op jit(solution)/shard_map/pallas_call | solution.py:309
  1.2 3.1 %collective-permute-start = (bf16[16,2176]{1,0:T(8,128)(2,1)S(1)}, bf16[16,2176]{1,0:T(8,128)(2,1)S(1)}, u32[]{:S(2)}, u32[]{:S(2)}) collective-permute-start(bf16[16,2176]{1,0:T(8,128)(2,1)S(1)} %get-tuple-element.28), channel_id=1, source_target_pairs={{0,2},{1,3},{2,0},{3,1},{4,6},{5,7},{6,4},{7,5},{8,10},{9,11},{10,... | collective-permute-start | bytes 208904 | tf_op jit(solution)/shard_map/ppermute | solution.py:328
  4.2 1.6 %collective-permute-start.1 = (bf16[16,2176]{1,0:T(8,128)(2,1)S(1)}, bf16[16,2176]{1,0:T(8,128)(2,1)S(1)}, u32[]{:S(2)}, u32[]{:S(2)}) collective-permute-start(bf16[16,2176]{1,0:T(8,128)(2,1)S(1)} %get-tuple-element.29), channel_id=1, source_target_pairs={{0,4},{1,5},{2,6},{3,7},{4,0},{5,1},{6,2},{7,3},{8,12},{9,13},{10,... | collective-permute-start | bytes 208904 | tf_op jit(solution)/shard_map/ppermute | solution.py:328
  5.8 0.0 collective-permute-start.2
  5.8 3.0 %collective-permute-start.3 = (bf16[16,2176]{1,0:T(8,128)(2,1)S(1)}, bf16[16,2176]{1,0:T(8,128)(2,1)S(1)}, u32[]{:S(2)}, u32[]{:S(2)}) collective-permute-start(bf16[16,2176]{1,0:T(8,128)(2,1)S(1)} %get-tuple-element.31), channel_id=1, source_target_pairs={{0,8},{1,9},{2,10},{3,11},{4,12},{5,13},{6,14},{7,15},{8,0},{9,1},... | collective-permute-start | bytes 208904 | tf_op jit(solution)/shard_map/ppermute | solution.py:328
  8.8 1.3 %collective-permute-start.4 = (bf16[16,2176]{1,0:T(8,128)(2,1)S(1)}, bf16[16,2176]{1,0:T(8,128)(2,1)S(1)}, u32[]{:S(2)}, u32[]{:S(2)}) collective-permute-start(bf16[16,2176]{1,0:T(8,128)(2,1)S(1)} %get-tuple-element.32), channel_id=1, source_target_pairs={{0,10},{1,11},{2,8},{3,9},{4,14},{5,15},{6,12},{7,13},{8,2},{9,3},... | collective-permute-start | bytes 208904 | tf_op jit(solution)/shard_map/ppermute | solution.py:328
  10.1 0.0 collective-permute-done.rest_1_
  10.1 3.6 %collective-permute-start.5 = (bf16[16,2176]{1,0:T(8,128)(2,1)S(1)}, bf16[16,2176]{1,0:T(8,128)(2,1)S(1)}, u32[]{:S(2)}, u32[]{:S(2)}) collective-permute-start(bf16[16,2176]{1,0:T(8,128)(2,1)S(1)} %get-tuple-element.33), channel_id=1, source_target_pairs={{0,12},{1,13},{2,14},{3,15},{4,8},{5,9},{6,10},{7,11},{8,4},{9,5},... | collective-permute-start | bytes 208904 | tf_op jit(solution)/shard_map/ppermute | solution.py:328
  13.7 0.0 collective-permute-done.1.rest_2_
  13.7 0.0 collective-permute-start.6
  13.7 0.0 collective-permute-done.2.rest_3_
  13.7 0.0 collective-permute-done.3.rest_4_
  13.7 5.8 %collective-permute-done.4.rest_5_ = bf16[16,2176]{1,0:T(8,128)(2,1)S(1)} collective-permute-done((bf16[16,2176]{1,0:T(8,128)(2,1)S(1)}, bf16[16,2176]{1,0:T(8,128)(2,1)S(1)}, u32[]{:S(2)}, u32[]{:S(2)}) %collective-permute-start.4) | collective-permute-done | bytes 69664 | tf_op jit(solution)/shard_map/ppermute | solution.py:328
  19.5 0.0 collective-permute-done.5.rest_6_
  19.5 1.3 %collective-permute-done.6.rest_7_ = bf16[16,2176]{1,0:T(8,128)(2,1)S(1)} collective-permute-done((bf16[16,2176]{1,0:T(8,128)(2,1)S(1)}, bf16[16,2176]{1,0:T(8,128)(2,1)S(1)}, u32[]{:S(2)}, u32[]{:S(2)}) %collective-permute-start.6) | collective-permute-done | bytes 69664 | tf_op jit(solution)/shard_map/ppermute | solution.py:328
  20.8 0.1 collective-permute-start.7
  20.9 0.0 copy-start
  20.9 4.6 %shard_map.93 = (bf16[8,192,128]{2,1,0:T(8,128)(2,1)S(1)}, bf16[8,192,128]{2,1,0:T(8,128)(2,1)S(1)}, bf16[2,192,128]{2,1,0:T(8,128)(2,1)S(1)}, bf16[2,192,128]{2,1,0:T(8,128)(2,1)S(1)}, f32[10,256]{1,0:T(8,128)S(1)}) custom-call(bf16[8,33]{1,0:T(8,128)(2,1)S(1)} %get-tuple-element.35.row_taps, bf16[8,33]{1,0:T(8,128)(2,1)S(1)} %get-tuple-element.36.column_taps, ...), custom_call_target="tpu_custom_call" | custom-call | flops 1000000000 | bytes 8000000 | tf_op jit(solution)/shard_map/pallas_call | solution.py:340
  25.6 0.0 collective-permute-done.7.rest_8_
  25.6 0.0 copy-done
  25.6 3.9 %shard_map.94 = (f32[256,1024]{1,0:T(8,128)S(1)}, f32[16,2,128]{2,1,0:T(2,128)S(1)}) custom-call(bf16[16,2176]{1,0:T(8,128)(2,1)S(1)} %get-tuple-element.27.rest_0_, bf16[16,2176]{1,0:T(8,128)(2,1)S(1)} %collective-permute-done.rest_1_, bf16[16,2176]{1,0:T(8,128)(2,1)S(1)} %collective-permute-done.1.rest_2_, ...), custom_call_target="tpu_custom_call" | custom-call | flops 4000000000 | bytes 8000000 | tf_op jit(solution)/shard_map/pallas_call | solution.py:352
  29.5 11.2 %all_to_all.5.sums = f32[16,2,128]{2,1,0:T(2,128)S(1)} all-to-all(f32[16,2,128]{2,1,0:T(2,128)S(1)} %get-tuple-element.48), channel_id=1, replica_groups=mesh['swath'=2,'band'=16] {'band'}, dimensions={0} | all-to-all | bytes 32768 | tf_op jit(solution)/shard_map/all_to_all | solution.py:367
  40.7 1.1 %shard_map.95 = bf16[256,1024]{1,0:T(8,128)(2,1)} custom-call(f32[256,1024]{1,0:T(8,128)S(1)} %get-tuple-element.47.filtered, f32[16,2,128]{2,1,0:T(2,128)S(1)} %all_to_all.5.sums, f32[10,256]{1,0:T(8,128)S(1)} %get-tuple-element.46.rest_13_.scales), custom_call_target="tpu_custom_call" | custom-call | tf_op jit(solution)/shard_map/pallas_call | solution.py:368
  (1 shorter events, 0.0 us)
Async XLA Ops:
  1.2 8.9 %collective-permute-start = (bf16[16,2176]{1,0:T(8,128)(2,1)S(1)}, bf16[16,2176]{1,0:T(8,128)(2,1)S(1)}, u32[]{:S(2)}, u32[]{:S(2)}) collective-permute-start(bf16[16,2176]{1,0:T(8,128)(2,1)S(1)} %get-tuple-element.28), channel_id=1, source_target_pairs={{0,2},{1,3},{2,0},{3,1},{4,6},{5,7},{6,4},{7,5},{8,10},{9,11},{10,... | collective-permute-start | bytes 208904 | tf_op jit(solution)/shard_map/ppermute | solution.py:328
  4.2 9.5 %collective-permute-start.1 = (bf16[16,2176]{1,0:T(8,128)(2,1)S(1)}, bf16[16,2176]{1,0:T(8,128)(2,1)S(1)}, u32[]{:S(2)}, u32[]{:S(2)}) collective-permute-start(bf16[16,2176]{1,0:T(8,128)(2,1)S(1)} %get-tuple-element.29), channel_id=1, source_target_pairs={{0,4},{1,5},{2,6},{3,7},{4,0},{5,1},{6,2},{7,3},{8,12},{9,13},{10,... | collective-permute-start | bytes 208904 | tf_op jit(solution)/shard_map/ppermute | solution.py:328
  5.8 7.9 %collective-permute-start.2 = (bf16[16,2176]{1,0:T(8,128)(2,1)S(1)}, bf16[16,2176]{1,0:T(8,128)(2,1)S(1)}, u32[]{:S(2)}, u32[]{:S(2)}) collective-permute-start(bf16[16,2176]{1,0:T(8,128)(2,1)S(1)} %get-tuple-element.30), channel_id=1, source_target_pairs={{0,6},{1,7},{2,4},{3,5},{4,2},{5,3},{6,0},{7,1},{8,14},{9,15},{10,... | collective-permute-start | bytes 208904 | tf_op jit(solution)/shard_map/ppermute | solution.py:328
  5.8 7.9 %collective-permute-start.3 = (bf16[16,2176]{1,0:T(8,128)(2,1)S(1)}, bf16[16,2176]{1,0:T(8,128)(2,1)S(1)}, u32[]{:S(2)}, u32[]{:S(2)}) collective-permute-start(bf16[16,2176]{1,0:T(8,128)(2,1)S(1)} %get-tuple-element.31), channel_id=1, source_target_pairs={{0,8},{1,9},{2,10},{3,11},{4,12},{5,13},{6,14},{7,15},{8,0},{9,1},... | collective-permute-start | bytes 208904 | tf_op jit(solution)/shard_map/ppermute | solution.py:328
  8.8 10.7 %collective-permute-start.4 = (bf16[16,2176]{1,0:T(8,128)(2,1)S(1)}, bf16[16,2176]{1,0:T(8,128)(2,1)S(1)}, u32[]{:S(2)}, u32[]{:S(2)}) collective-permute-start(bf16[16,2176]{1,0:T(8,128)(2,1)S(1)} %get-tuple-element.32), channel_id=1, source_target_pairs={{0,10},{1,11},{2,8},{3,9},{4,14},{5,15},{6,12},{7,13},{8,2},{9,3},... | collective-permute-start | bytes 208904 | tf_op jit(solution)/shard_map/ppermute | solution.py:328
  10.1 9.4 %collective-permute-start.5 = (bf16[16,2176]{1,0:T(8,128)(2,1)S(1)}, bf16[16,2176]{1,0:T(8,128)(2,1)S(1)}, u32[]{:S(2)}, u32[]{:S(2)}) collective-permute-start(bf16[16,2176]{1,0:T(8,128)(2,1)S(1)} %get-tuple-element.33), channel_id=1, source_target_pairs={{0,12},{1,13},{2,14},{3,15},{4,8},{5,9},{6,10},{7,11},{8,4},{9,5},... | collective-permute-start | bytes 208904 | tf_op jit(solution)/shard_map/ppermute | solution.py:328
  13.7 7.1 %collective-permute-start.6 = (bf16[16,2176]{1,0:T(8,128)(2,1)S(1)}, bf16[16,2176]{1,0:T(8,128)(2,1)S(1)}, u32[]{:S(2)}, u32[]{:S(2)}) collective-permute-start(bf16[16,2176]{1,0:T(8,128)(2,1)S(1)} %get-tuple-element.34), channel_id=1, source_target_pairs={{0,14},{1,15},{2,12},{3,13},{4,10},{5,11},{6,8},{7,9},{8,6},{9,7},... | collective-permute-start | bytes 208904 | tf_op jit(solution)/shard_map/ppermute | solution.py:328
  20.8 4.7 %collective-permute-start.7 = (bf16[128,1152]{1,0:T(8,128)(2,1)S(1)}, bf16[128,1152]{1,0:T(8,128)(2,1)S(1)}, u32[]{:S(2)}, u32[]{:S(2)}) collective-permute-start(bf16[128,1152]{1,0:T(8,128)(2,1)S(1)} %shard_map.92), channel_id=1, source_target_pairs={{0,1},{1,0},{2,3},{3,2},{4,5},{5,4},{6,7},{7,6},{8,9},{9,8},{10,11... | collective-permute-start | bytes 884744 | tf_op jit(solution)/shard_map/ppermute | solution.py:337
  20.9 4.7 %copy-start = (bf16[256,1024]{1,0:T(8,128)(2,1)S(1)}, bf16[256,1024]{1,0:T(8,128)(2,1)}, u32[]{:S(2)}) copy-start(bf16[256,1024]{1,0:T(8,128)(2,1)} %rest_14_.1) | copy-start | bytes 1572868

commit v5 on v4

--- a/solution.py
+++ b/solution.py
@@ -139,12 +139,9 @@
             tile = jnp.where(lane >= start if start >= 0 else lane < LANES + start, tile, 0.0)
             bank[at, 16 * m : 16 * (m + 1), :] = tile.astype(jnp.bfloat16)
 
-    def per_kernel(k, carry):
-        fill(rows, k, tap_rows[pl.ds(k, 1), :])
-        fill(columns, k, tap_cols[pl.ds(k, 1), :])
-        return carry
-
-    lax.fori_loop(0, plan.kernels, per_kernel, 0)
+    for k in range(plan.kernels):
+        fill(rows, k, tap_rows[k : k + 1, :])
+        fill(columns, k, tap_cols[k : k + 1, :])
 
     def column(line):
         count = line.shape[1]
@@ -290,7 +287,8 @@
 
 
 def hops(chips):
-    return sorted(range(1, chips), key=lambda hop: (-hop.bit_length(), hop))
+    half = chips // 2
+    return sorted(range(1, chips), key=lambda hop: (hop < half, (hop & 1) ^ (hop < half), -hop))
 
 
 def on_device(

time: 41.9 us -> 40.8 us (0.974)
  Pallas kernels: 10.8 us -> 9.64 us
    pallas_call x1, Pallas kernels: 4.63 us -> 3.46 us  [on_device(): pl.pallas_call(functools.partial(bank_kernel, plan), out_shape=[bank(kern...]
  transfers between devices with their start and end apart: 8 -> 8, of which waited for: 2 -> 2; matrix products, arithmetic and copies ran while one was open for 0% -> 0% of each run, Pallas kernels for 11% -> 9%
where the time goes in v5:
time: 40.8 us; the launch traced here: 40.6 us
  starting transfers between devices  12.6 us (31%)
  blocking collectives  11.2 us (27%)
  Pallas kernels  9.64 us (24%)
  waiting for transfers between devices  7.1 us (17%)
    ppermute x7, starting transfers between devices, on_device(): unions[hop] = lax.ppermute(unions[hop], 'band', pairs)  12.5 us
    all_to_all x1, blocking collectives, on_device(): sums = lax.all_to_all(sums, 'band', 0, 0, tiled=True)  11.2 us
    ppermute x7, waiting for transfers between devices, on_device(): unions[hop] = lax.ppermute(unions[hop], 'band', pairs)  7.1 us
    pallas_call x1, Pallas kernels, on_device(): pl.pallas_call(functools.partial(main_kernel, plan), out_shape=[pltpu.VME...  3.88 us
    pallas_call x1, Pallas kernels, on_device(): pl.pallas_call(functools.partial(bank_kernel, plan), out_shape=[bank(kern...  3.46 us
    pallas_call x1, Pallas kernels, on_device(): pl.pallas_call(functools.partial(send_kernel, plan), out_shape=[pltpu.VME...  1.17 us
    pallas_call x1, Pallas kernels, on_device(): pl.pallas_call(functools.partial(last_kernel, plan), out_shape=jax.ShapeD...  1.08 us
  transfers between devices with their start and end apart: 8, of which 2 were waited for; matrix products, arithmetic and copies ran while one was open for 0% of the time, Pallas kernels for 9%

profile of v5, /device:TPU:0, one launch (start us, length us, event | category | flops | bytes accessed | tf_op | source)
XLA Modules:
  0.0 40.6 jit_solution(15173765228893753382)
XLA Ops:
  0.0 1.2 %shard_map.91 = (bf16[16,2176]{1,0:T(8,128)(2,1)S(1)}, bf16[16,2176]{1,0:T(8,128)(2,1)S(1)}, bf16[16,2176]{1,0:T(8,128)(2,1)S(1)}, bf16[16,2176]{1,0:T(8,128)(2,...) custom-call(bf16[16,16384]{1,0:T(8,128)(2,1)} %design.1, ...), custom_call_target="tpu_custom_call" | custom-call | tf_op jit(solution)/shard_map/pallas_call | solution.py:307
  1.2 3.1 %collective-permute-start = (bf16[16,2176]{1,0:T(8,128)(2,1)S(1)}, bf16[16,2176]{1,0:T(8,128)(2,1)S(1)}, u32[]{:S(2)}, u32[]{:S(2)}) collective-permute-start(bf16[16,2176]{1,0:T(8,128)(2,1)S(1)} %get-tuple-element.28), channel_id=1, source_target_pairs={{0,2},{1,3},{2,0},{3,1},{4,6},{5,7},{6,4},{7,5},{8,10},{9,11},{10,... | collective-permute-start | bytes 208904 | tf_op jit(solution)/shard_map/ppermute | solution.py:326
  4.2 1.6 %collective-permute-start.1 = (bf16[16,2176]{1,0:T(8,128)(2,1)S(1)}, bf16[16,2176]{1,0:T(8,128)(2,1)S(1)}, u32[]{:S(2)}, u32[]{:S(2)}) collective-permute-start(bf16[16,2176]{1,0:T(8,128)(2,1)S(1)} %get-tuple-element.29), channel_id=1, source_target_pairs={{0,4},{1,5},{2,6},{3,7},{4,0},{5,1},{6,2},{7,3},{8,12},{9,13},{10,... | collective-permute-start | bytes 208904 | tf_op jit(solution)/shard_map/ppermute | solution.py:326
  5.8 0.0 collective-permute-start.2
  5.8 3.0 %collective-permute-start.3 = (bf16[16,2176]{1,0:T(8,128)(2,1)S(1)}, bf16[16,2176]{1,0:T(8,128)(2,1)S(1)}, u32[]{:S(2)}, u32[]{:S(2)}) collective-permute-start(bf16[16,2176]{1,0:T(8,128)(2,1)S(1)} %get-tuple-element.31), channel_id=1, source_target_pairs={{0,8},{1,9},{2,10},{3,11},{4,12},{5,13},{6,14},{7,15},{8,0},{9,1},... | collective-permute-start | bytes 208904 | tf_op jit(solution)/shard_map/ppermute | solution.py:326
  8.8 1.3 %collective-permute-start.4 = (bf16[16,2176]{1,0:T(8,128)(2,1)S(1)}, bf16[16,2176]{1,0:T(8,128)(2,1)S(1)}, u32[]{:S(2)}, u32[]{:S(2)}) collective-permute-start(bf16[16,2176]{1,0:T(8,128)(2,1)S(1)} %get-tuple-element.32), channel_id=1, source_target_pairs={{0,10},{1,11},{2,8},{3,9},{4,14},{5,15},{6,12},{7,13},{8,2},{9,3},... | collective-permute-start | bytes 208904 | tf_op jit(solution)/shard_map/ppermute | solution.py:326
  10.1 0.0 collective-permute-done.rest_1_
  10.1 3.6 %collective-permute-start.5 = (bf16[16,2176]{1,0:T(8,128)(2,1)S(1)}, bf16[16,2176]{1,0:T(8,128)(2,1)S(1)}, u32[]{:S(2)}, u32[]{:S(2)}) collective-permute-start(bf16[16,2176]{1,0:T(8,128)(2,1)S(1)} %get-tuple-element.33), channel_id=1, source_target_pairs={{0,12},{1,13},{2,14},{3,15},{4,8},{5,9},{6,10},{7,11},{8,4},{9,5},... | collective-permute-start | bytes 208904 | tf_op jit(solution)/shard_map/ppermute | solution.py:326
  13.7 0.0 collective-permute-done.1.rest_2_
  13.7 0.0 collective-permute-start.6
  13.7 0.0 collective-permute-done.2.rest_3_
  13.7 0.0 collective-permute-done.3.rest_4_
  13.7 5.8 %collective-permute-done.4.rest_5_ = bf16[16,2176]{1,0:T(8,128)(2,1)S(1)} collective-permute-done((bf16[16,2176]{1,0:T(8,128)(2,1)S(1)}, bf16[16,2176]{1,0:T(8,128)(2,1)S(1)}, u32[]{:S(2)}, u32[]{:S(2)}) %collective-permute-start.4) | collective-permute-done | bytes 69664 | tf_op jit(solution)/shard_map/ppermute | solution.py:326
  19.5 0.0 collective-permute-done.5.rest_6_
  19.5 1.3 %collective-permute-done.6.rest_7_ = bf16[16,2176]{1,0:T(8,128)(2,1)S(1)} collective-permute-done((bf16[16,2176]{1,0:T(8,128)(2,1)S(1)}, bf16[16,2176]{1,0:T(8,128)(2,1)S(1)}, u32[]{:S(2)}, u32[]{:S(2)}) %collective-permute-start.6) | collective-permute-done | bytes 69664 | tf_op jit(solution)/shard_map/ppermute | solution.py:326
  20.8 0.1 collective-permute-start.7
  20.9 0.0 copy-start
  20.9 3.5 %shard_map.93 = (bf16[8,192,128]{2,1,0:T(8,128)(2,1)S(1)}, bf16[8,192,128]{2,1,0:T(8,128)(2,1)S(1)}, bf16[2,192,128]{2,1,0:T(8,128)(2,1)S(1)}, bf16[2,192,128]{2,1,0:T(8,128)(2,1)S(1)}, f32[10,256]{1,0:T(8,128)S(1)}) custom-call(bf16[8,33]{1,0:T(8,128)(2,1)S(1)} %get-tuple-element.35.row_taps, bf16[8,33]{1,0:T(8,128)(2,1)S(1)} %get-tuple-element.36.column_taps, ...), custom_call_target="tpu_custom_call" | custom-call | flops 1000000000 | bytes 8000000 | tf_op jit(solution)/shard_map/pallas_call | solution.py:338
  24.4 0.0 collective-permute-done.7.rest_8_
  24.4 0.0 copy-done
  24.4 3.9 %shard_map.94 = (f32[256,1024]{1,0:T(8,128)S(1)}, f32[16,2,128]{2,1,0:T(2,128)S(1)}) custom-call(bf16[16,2176]{1,0:T(8,128)(2,1)S(1)} %get-tuple-element.27.rest_0_, bf16[16,2176]{1,0:T(8,128)(2,1)S(1)} %collective-permute-done.rest_1_, bf16[16,2176]{1,0:T(8,128)(2,1)S(1)} %collective-permute-done.1.rest_2_, ...), custom_call_target="tpu_custom_call" | custom-call | flops 4000000000 | bytes 8000000 | tf_op jit(solution)/shard_map/pallas_call | solution.py:350
  28.3 11.2 %all_to_all.5.sums = f32[16,2,128]{2,1,0:T(2,128)S(1)} all-to-all(f32[16,2,128]{2,1,0:T(2,128)S(1)} %get-tuple-element.48), channel_id=1, replica_groups=mesh['swath'=2,'band'=16] {'band'}, dimensions={0} | all-to-all | bytes 32768 | tf_op jit(solution)/shard_map/all_to_all | solution.py:365
  39.5 1.1 %shard_map.95 = bf16[256,1024]{1,0:T(8,128)(2,1)} custom-call(f32[256,1024]{1,0:T(8,128)S(1)} %get-tuple-element.47.filtered, f32[16,2,128]{2,1,0:T(2,128)S(1)} %all_to_all.5.sums, f32[10,256]{1,0:T(8,128)S(1)} %get-tuple-element.46.rest_13_.scales), custom_call_target="tpu_custom_call" | custom-call | tf_op jit(solution)/shard_map/pallas_call | solution.py:366
  (1 shorter events, 0.0 us)
Async XLA Ops:
  1.2 8.9 %collective-permute-start = (bf16[16,2176]{1,0:T(8,128)(2,1)S(1)}, bf16[16,2176]{1,0:T(8,128)(2,1)S(1)}, u32[]{:S(2)}, u32[]{:S(2)}) collective-permute-start(bf16[16,2176]{1,0:T(8,128)(2,1)S(1)} %get-tuple-element.28), channel_id=1, source_target_pairs={{0,2},{1,3},{2,0},{3,1},{4,6},{5,7},{6,4},{7,5},{8,10},{9,11},{10,... | collective-permute-start | bytes 208904 | tf_op jit(solution)/shard_map/ppermute | solution.py:326
  4.2 9.5 %collective-permute-start.1 = (bf16[16,2176]{1,0:T(8,128)(2,1)S(1)}, bf16[16,2176]{1,0:T(8,128)(2,1)S(1)}, u32[]{:S(2)}, u32[]{:S(2)}) collective-permute-start(bf16[16,2176]{1,0:T(8,128)(2,1)S(1)} %get-tuple-element.29), channel_id=1, source_target_pairs={{0,4},{1,5},{2,6},{3,7},{4,0},{5,1},{6,2},{7,3},{8,12},{9,13},{10,... | collective-permute-start | bytes 208904 | tf_op jit(solution)/shard_map/ppermute | solution.py:326
  5.8 7.9 %collective-permute-start.2 = (bf16[16,2176]{1,0:T(8,128)(2,1)S(1)}, bf16[16,2176]{1,0:T(8,128)(2,1)S(1)}, u32[]{:S(2)}, u32[]{:S(2)}) collective-permute-start(bf16[16,2176]{1,0:T(8,128)(2,1)S(1)} %get-tuple-element.30), channel_id=1, source_target_pairs={{0,6},{1,7},{2,4},{3,5},{4,2},{5,3},{6,0},{7,1},{8,14},{9,15},{10,... | collective-permute-start | bytes 208904 | tf_op jit(solution)/shard_map/ppermute | solution.py:326
  5.8 7.9 %collective-permute-start.3 = (bf16[16,2176]{1,0:T(8,128)(2,1)S(1)}, bf16[16,2176]{1,0:T(8,128)(2,1)S(1)}, u32[]{:S(2)}, u32[]{:S(2)}) collective-permute-start(bf16[16,2176]{1,0:T(8,128)(2,1)S(1)} %get-tuple-element.31), channel_id=1, source_target_pairs={{0,8},{1,9},{2,10},{3,11},{4,12},{5,13},{6,14},{7,15},{8,0},{9,1},... | collective-permute-start | bytes 208904 | tf_op jit(solution)/shard_map/ppermute | solution.py:326
  8.8 10.7 %collective-permute-start.4 = (bf16[16,2176]{1,0:T(8,128)(2,1)S(1)}, bf16[16,2176]{1,0:T(8,128)(2,1)S(1)}, u32[]{:S(2)}, u32[]{:S(2)}) collective-permute-start(bf16[16,2176]{1,0:T(8,128)(2,1)S(1)} %get-tuple-element.32), channel_id=1, source_target_pairs={{0,10},{1,11},{2,8},{3,9},{4,14},{5,15},{6,12},{7,13},{8,2},{9,3},... | collective-permute-start | bytes 208904 | tf_op jit(solution)/shard_map/ppermute | solution.py:326
  10.1 9.4 %collective-permute-start.5 = (bf16[16,2176]{1,0:T(8,128)(2,1)S(1)}, bf16[16,2176]{1,0:T(8,128)(2,1)S(1)}, u32[]{:S(2)}, u32[]{:S(2)}) collective-permute-start(bf16[16,2176]{1,0:T(8,128)(2,1)S(1)} %get-tuple-element.33), channel_id=1, source_target_pairs={{0,12},{1,13},{2,14},{3,15},{4,8},{5,9},{6,10},{7,11},{8,4},{9,5},... | collective-permute-start | bytes 208904 | tf_op jit(solution)/shard_map/ppermute | solution.py:326
  13.7 7.1 %collective-permute-start.6 = (bf16[16,2176]{1,0:T(8,128)(2,1)S(1)}, bf16[16,2176]{1,0:T(8,128)(2,1)S(1)}, u32[]{:S(2)}, u32[]{:S(2)}) collective-permute-start(bf16[16,2176]{1,0:T(8,128)(2,1)S(1)} %get-tuple-element.34), channel_id=1, source_target_pairs={{0,14},{1,15},{2,12},{3,13},{4,10},{5,11},{6,8},{7,9},{8,6},{9,7},... | collective-permute-start | bytes 208904 | tf_op jit(solution)/shard_map/ppermute | solution.py:326
  20.8 3.6 %collective-permute-start.7 = (bf16[128,1152]{1,0:T(8,128)(2,1)S(1)}, bf16[128,1152]{1,0:T(8,128)(2,1)S(1)}, u32[]{:S(2)}, u32[]{:S(2)}) collective-permute-start(bf16[128,1152]{1,0:T(8,128)(2,1)S(1)} %shard_map.92), channel_id=1, source_target_pairs={{0,1},{1,0},{2,3},{3,2},{4,5},{5,4},{6,7},{7,6},{8,9},{9,8},{10,11... | collective-permute-start | bytes 884744 | tf_op jit(solution)/shard_map/ppermute | solution.py:335
  20.9 3.5 %copy-start = (bf16[256,1024]{1,0:T(8,128)(2,1)S(1)}, bf16[256,1024]{1,0:T(8,128)(2,1)}, u32[]{:S(2)}) copy-start(bf16[256,1024]{1,0:T(8,128)(2,1)} %rest_14_.1) | copy-start | bytes 1572868
